TPU v7x, 256 devices: a whole 4x4x8 slice. The times are simulated.
256 devices in a mesh: len: 32 (over z, y), wid: 8 (over x, core).
Axes of the slice: x: 4, y: 4, z: 8, core: 2. Of those that a mesh axis runs over, the one named last changes fastest.
Arguments:
- positions: float32 [32, 8, 192, 3, 128], P('len', 'wid'), may hold values from 0 to 8
- velocities: float32 [32, 8, 192, 3, 128], P('len', 'wid'), may hold values from -4 to 4
- spins: float32 [32, 8, 192, 3, 128], P('len', 'wid'), may hold values from -4 to 4
- sphere_radii: float32 [32, 8, 192, 128], P('len', 'wid'), may hold values from 0.4 to 0.6
- swap_counts: int32 [32, 8, 8], P('len', 'wid'), may hold values from 0 to 24, as said below
- swap_slots: int32 [32, 8, 8, 24], P('len', 'wid'), may hold values from 0 to 191, as said below
- ghost_slots: int32 [32, 8, 4, 48], P('len', 'wid'), may hold values from 0 to 191, as said below
- corner_slots: int32 [32, 8, 4, 4], P('len', 'wid'), may hold values from 0 to 191, as said below
- pair_first: int32 [32, 8, 128], P('len', 'wid'), may hold values from 0 to 191
- pair_second: int32 [32, 8, 128], P('len', 'wid'), may hold values from 0 to 399, as said below
- pair_live: int32 [32, 8], P('len', 'wid'), may hold values from 1 to 128, as said below
Outputs:
- positions_out: float32 [32, 8, 192, 3, 128], P('len', 'wid')
- velocities_out: float32 [32, 8, 192, 3, 128], P('len', 'wid')
- spins_out: float32 [32, 8, 192, 3, 128], P('len', 'wid')
- sphere_radii_out: float32 [32, 8, 192, 128], P('len', 'wid')
Inputs may be any that keep to these rules, and one draw needn't show every extreme that they name: `swap_counts`: equal on the two partners of each step; some pair exchanges 24 blocks in every step. `swap_slots`: distinct within one device and step. `ghost_slots`: distinct within one device and direction. `corner_slots`: distinct within one device and direction. `pair_second`: never names a ghost block from a neighbour outside the grid. Only the first pair_live entries of a device's lists are used; some device uses all 128.
All inputs are finite; a program needn't handle non-finite values.
Results may differ from a plain program's by a relative error of at most 0.0003.
Values sent between devices are 32-bit elements; how exact they have to be, the bound alone decides.
No kernel may reach another device: no remote copies, remote signals or barrier semaphores. Data moves between devices by JAX's collectives and lax.ppermute only.
A program may use at most 64 MiB of HBM per device.

v0:
```python
import functools
import math

import jax
import jax.numpy as jnp
from jax import lax
from jax.experimental import pallas as pl
from jax.experimental.pallas import tpu as pltpu
from jax.sharding import PartitionSpec as P

DENSITY = 1.9
TIME_STEP = 0.01
BLK = 128
S = 192
MOVE = 24
GHOST = 48
CORNER = 4
PAIRS = 128
BITS = 8
LBITS = 5
ROWS = 10
OWN = S
RECV = MOVE * BITS
WIDE = GHOST + 2 * CORNER
CORNERS = 2 * CORNER
G_WA, G_WB, G_LA, G_LB, G_CA, G_CB = 0, GHOST, 2 * GHOST, 3 * GHOST, 4 * GHOST, 4 * GHOST + CORNERS
GBASE = OWN + RECV
T_SEND, T_FINAL, T_GHOST, T_CORNER = 0, 192, 384, 576
T_SIZE = 640
Q_A, Q_B, Q_SLOT, Q_END = 0, 136, 272, 408
Q_SIZE = 512
CAPS = {2: 16, 3: 32, 4: 32, 6: 24, 7: 24}
CATS = 12
SPARE = 11
MARGIN = 0.02
UNROLL = 3

SMEM = pl.BlockSpec(memory_space=pltpu.SMEM)
VMEM = pl.BlockSpec(memory_space=pltpu.VMEM)
HBM = pl.BlockSpec(memory_space=pltpu.HBM)
ANY = pl.BlockSpec(memory_space=pl.ANY)


def f32(*shape):
    return jax.ShapeDtypeStruct(shape, jnp.float32)


def vmem(*shape):
    return pltpu.VMEM(shape, jnp.float32)


def call(body, out_shape, in_specs, out_specs, scratch=(), name=None, flops=0):
    return pl.pallas_call(
        body,
        out_shape=out_shape,
        in_specs=in_specs,
        out_specs=out_specs,
        scratch_shapes=list(scratch),
        name=name,
        compiler_params=pltpu.CompilerParams(vmem_limit_bytes=24 * 1024 * 1024),
        cost_estimate=pl.CostEstimate(flops=flops, transcendentals=0, bytes_accessed=1000000),
    )


def pack_kernel(slots_hbm, pos, vel, spin, rad, pool, send, slots, sems):
    copies = [
        pltpu.make_async_copy(slots_hbm, slots, sems.at[0]),
        pltpu.make_async_copy(pos, pool.at[0:3], sems.at[1]),
        pltpu.make_async_copy(vel, pool.at[3:6], sems.at[2]),
        pltpu.make_async_copy(spin, pool.at[6:9], sems.at[3]),
        pltpu.make_async_copy(rad, pool.at[9], sems.at[4]),
    ]
    for copy in copies:
        copy.start()
    for copy in copies:
        copy.wait()
    for j in range(MOVE):
        s = slots[0, j]
        for c in range(ROWS):
            send[c, j : j + 1, :] = pool[c, pl.ds(s, 1), :]


def table_kernel(counts, slots, ghosts, corners, tab, code):
    def init(i, _):
        for k in range(16):
            code[16 * i + k] = 16 * i + k
        return 0

    lax.fori_loop(0, S // 16, init, 0)

    def move(t, _):
        live = counts[t]

        def one(i, _):
            first = 8 * i
            places = [slots[t, first + k] for k in range(8)]
            olds = [code[s] for s in places]
            for k in range(8):
                tab[T_SEND + MOVE * t + first + k] = olds[k]
            for k in range(8):
                j = first + k
                code[places[k]] = jnp.where(j < live, S + MOVE * t + j, olds[k])
            return 0

        lax.fori_loop(0, MOVE // 8, one, 0)
        return 0

    lax.fori_loop(0, BITS, move, 0)

    def final(i, _):
        values = [code[8 * i + k] for k in range(8)]
        for k in range(8):
            tab[T_FINAL + 8 * i + k] = values[k]
        return 0

    lax.fori_loop(0, S // 8, final, 0)
    for k in range(4):

        def face(i, _, k=k):
            values = [code[ghosts[k, 8 * i + g]] for g in range(8)]
            for g in range(8):
                tab[T_GHOST + GHOST * k + 8 * i + g] = values[g]
            return 0

        lax.fori_loop(0, GHOST // 8, face, 0)
        for g in range(CORNER):
            tab[T_CORNER + CORNER * k + g] = code[corners[k, g]]


def order_kernel(tab, first, second, live_ref, out, cat, start):
    live = live_ref[0, 0]
    even_w = odd("wid") == 0
    even_l = odd("len") == 0
    for k in range(CATS):
        start[k] = 0
    groups = (live + 3) // 4

    def sort_in(i, _):
        cats = []
        for k in range(4):
            e = 4 * i + k
            b = second[e]
            code = jnp.maximum(tab[T_FINAL + first[e]], tab[T_FINAL + jnp.minimum(b, S - 1)])
            ready = jnp.where(code < S, 0, ((code - S) * 171 >> 12) + 1)
            g = b - S
            wide = (g >= GHOST) & (g < 3 * GHOST)
            where = jnp.where(b < S, ready, jnp.where(wide, 9, 10))
            cats.append(jnp.where(e < live, where, SPARE))
        for k in range(4):
            cat[4 * i + k] = cats[k]
        for k in range(4):
            start[cats[k]] = start[cats[k]] + 1
        return 0

    lax.fori_loop(0, groups, sort_in, 0)
    total = jnp.int32(0)
    done = jnp.int32(0)
    for k in range(CATS):
        n = start[k]
        start[k] = total
        total = total + n
        if k < BITS:
            done = jnp.minimum(total, done + CAPS.get(k, 0))
            out[Q_END + k] = done
        else:
            out[Q_END + k] = total

    def place(i, _):
        spots = []
        for k in range(4):
            e = 4 * i + k
            a = first[e]
            b = second[e]
            g = b - S
            h = g - 4 * GHOST
            diagonal = h >= 0
            face = jnp.where(g < GHOST, 0, jnp.where(g < 2 * GHOST, 1, jnp.where(g < 3 * GHOST, 2, 3)))
            low = jnp.where(diagonal, h < 2 * CORNER, face < 2)
            wide = (face == 1) | (face == 2)
            ahead = jnp.where(wide & (h < 0), low == even_w, low == even_l)
            start_at = jnp.where(wide, G_WA, G_LA) + jnp.where(ahead, 0, GHOST) + g - face * GHOST
            corner_at = G_CA + jnp.where(ahead, 0, CORNERS) + h - jnp.where(low, 0, CORNERS)
            ghost = jnp.where(diagonal, corner_at, start_at) + GBASE
            own = tab[T_FINAL + jnp.minimum(b, S - 1)]
            spots.append((cat[e], a, tab[T_FINAL + a], jnp.where(b < S, own, ghost)))
        for where, a, near, far in spots:
            at = start[where]
            start[where] = at + 1
            out[Q_SLOT + at] = a
            out[Q_A + at] = near
            out[Q_B + at] = far
        return 0

    lax.fori_loop(0, groups, place, 0)


def gather_rows(everything, tab, base, count, out, at):
    for j in range(count):
        s = tab[base + j]
        for c in range(ROWS):
            out[c, at + j : at + j + 1, :] = everything[c, pl.ds(s, 1), :]


def fill(everything, pool, received):
    everything[:, 0:OWN, :] = pool[...]
    for k, part in enumerate(received):
        everything[:, OWN + MOVE * k : OWN + MOVE * (k + 1), :] = part[...]


def step_kernel(t, tab, pool, *rest):
    received, send, everything = rest[:t], rest[-2], rest[-1]
    fill(everything, pool, received)
    gather_rows(everything, tab, T_SEND + MOVE * t, MOVE, send, 0)


def odd(axis):
    return lax.rem(lax.axis_index(axis), 2)


def ghost_kernel(tab, pool, *rest):
    received = rest[:BITS]
    la, lb, wa, wb, everything = rest[-5:]
    fill(everything, pool, received)
    up = 1 - odd("wid")
    for out, k in ((wa, up), (wb, 1 - up)):
        gather_rows(everything, tab, T_GHOST + GHOST * (1 + k), GHOST, out, 0)
        gather_rows(everything, tab, T_CORNER + CORNER * k, CORNER, out, GHOST)
        gather_rows(everything, tab, T_CORNER + CORNER * (2 + k), CORNER, out, GHOST + CORNER)
    up = 1 - odd("len")
    for out, k in ((la, up), (lb, 1 - up)):
        gather_rows(everything, tab, T_GHOST + 3 * GHOST * k, GHOST, out, 0)


def corner_kernel(wa, wb, _, ca, cb):
    up = 1 - odd("len")
    flip = odd("wid")
    swap = jnp.full((CORNER, BLK), flip) == 1
    for out, k in ((ca, up), (cb, 1 - up)):
        for c in range(ROWS):
            at = pl.ds(GHOST + CORNER * k, CORNER)
            a, b = wa[c, at, :], wb[c, at, :]
            out[c, 0:CORNER, :] = jnp.where(swap, b, a)
            out[c, CORNER:CORNERS, :] = jnp.where(swap, a, b)


def rounded(x):
    return x.astype(jnp.bfloat16).astype(jnp.float32)


def factor(x, y, z, a, sub, near):
    pick = (sub & 1) == 0 if near else (sub & 2) == 0
    out = []
    for v in (jnp.where(sub < 4, x, y), jnp.where(sub < 4, z, a)):
        high = rounded(v)
        w = jnp.where(pick, high, v - high)
        out.append(w + w if near else w)
    c = a * a - ((x * x + y * y) + z * z)
    if near:
        c = c + MARGIN
    c1 = rounded(c)
    rest = c - c1
    c2 = rounded(rest)
    c3 = rest - c2
    b = 3 if near else 0
    ones = sub < 3 if near else (sub >= 3) & (sub < 6)
    tail = jnp.where(sub == b + 2, c3, jnp.where(ones, 1.0, 0.0))
    out.append(jnp.where(sub == b, c1, jnp.where(sub == b + 1, c2, tail)))
    out.append(jnp.zeros_like(x))
    return jnp.concatenate(out, axis=0).astype(jnp.bfloat16)


def contact(near, far, touching):
    px, py, pz, vx, vy, vz, sx, sy, sz, a = near
    qx, qy, qz, ux, uy, uz, tx, ty, tz, b = far
    rx, ry, rz = qx - px, qy - py, qz - pz
    d2 = (rx * rx + ry * ry) + (rz * rz + 0.01)
    inv = lax.rsqrt(d2)
    delta = jnp.maximum((a + b) - d2 * inv, 0.0)
    root = delta * lax.rsqrt(jnp.maximum(delta, 1e-30))
    nx, ny, nz = rx * inv, ry * inv, rz * inv
    wx, wy, wz = sx + tx, sy + ty, sz + tz
    dx, dy, dz = ux - vx, uy - vy, uz - vz
    ex = (dx - wy * nz) + wz * ny
    ey = (dy - wz * nx) + wx * nz
    ez = (dz - wx * ny) + wy * nx
    un = (ex * nx + ey * ny) + ez * nz
    g = jnp.where(touching, jnp.maximum(root * (30.0 * delta - un), 0.0), 0.0)
    gx, gy, gz = ex - un * nx, ey - un * ny, ez - un * nz
    c = g * lax.rsqrt((gx * gx + gy * gy) + (gz * gz + 0.01))
    cx, cy, cz = c * gx, c * gy, c * gz
    force = [cx, cy, cz, g * nx, g * ny, g * nz]
    return force + [ny * cz - nz * cy, nz * cx - nx * cz, nx * cy - ny * cx]


def eight_pairs(everything, nears, fars, used, near_s, far_s, words):
    sub = lax.broadcasted_iota(jnp.int32, (8, BLK), 0)

    def row(c, i):
        return jnp.broadcast_to(everything[c, pl.ds(i, 1), :], (8, BLK))

    for u in range(8):
        a, b = nears[u], fars[u]
        for c in range(ROWS):
            near_s[c, u : u + 1, :] = everything[c, pl.ds(a, 1), :]
            far_s[c, u : u + 1, :] = everything[c, pl.ds(b, 1), :]
        left = factor(*[row(c, b) for c in (0, 1, 2, 9)], sub, False)
        right = factor(*[row(c, a) for c in (0, 1, 2, 9)], sub, True)
        reach = lax.dot_general(
            left, right, (((0,), (0,)), ((), ())), preferred_element_type=jnp.float32
        )
        word = None
        for m in range(BLK // 8):
            bit = jnp.where(reach[8 * m : 8 * m + 8] > 0.0, 1 << m, 0)
            word = bit if word is None else word | bit
        word = word | (pltpu.roll(word, 4, 0) << 16)
        words[8 * u : 8 * u + 8, :] = word & used[u]
    left_over = [words[pl.ds(q, 8, stride=8), :] for q in range(4)]
    most = jnp.max(sum(lax.population_count(w) for w in left_over))

    def turned(x):
        return x[:6] + [x[6] * x[9], x[7] * x[9], x[8] * x[9], x[9]]

    near = turned([near_s[c] for c in range(ROWS)])
    far = turned([far_s[c] for c in range(ROWS)])

    def some(_, carry):
        w, acc = list(carry[:4]), list(carry[4:])
        for _ in range(UNROLL):
            some_in = [x != 0 for x in w[:3]]
            word = jnp.where(some_in[0], w[0], jnp.where(some_in[1], w[1], jnp.where(some_in[2], w[2], w[3])))
            q = jnp.where(some_in[0], 0, jnp.where(some_in[1], 1, jnp.where(some_in[2], 2, 3)))
            low = word & (-word)
            bit = 31 - lax.clz(low)
            w = [jnp.where(q == i, x ^ low, x) for i, x in enumerate(w)]
            j = (((bit & 15) << 3) + q + ((bit >> 4) << 2)) & (BLK - 1)
            terms = contact(near, [jnp.take_along_axis(x, j, axis=1) for x in far], low != 0)
            acc = [x + y for x, y in zip(acc, terms)]
        return (*w, *acc)

    zero = jnp.zeros((8, BLK), jnp.float32)
    passes = (most + UNROLL - 1) // UNROLL
    acc = lax.fori_loop(0, passes, some, (*left_over, *([zero] * 9)))[4:]
    force = [10.0 * acc[k] - 20.0 * acc[3 + k] for k in range(3)]
    scale = 10.0 * near[9]
    return force + [scale * acc[6 + k] for k in range(3)]


def all_pairs(everything, pairs, near_base, low, high, shift, scratch, sink):
    def group(i, _):
        at = [low + 8 * i + u for u in range(8)]
        inside = [jnp.minimum(e, high - 1) for e in at]
        used = [jnp.where(e < high, -1, 0) for e in at]
        nears = [pairs[near_base + e] for e in inside]
        fars = [pairs[Q_B + e] - shift for e in inside]
        sink(i, inside, eight_pairs(everything, nears, fars, used, *scratch))
        return 0

    lax.fori_loop(0, (high - low + 7) // 8, group, 0)


def early_kernel(t, pairs, pool, *rest):
    received, rows, everything, scratch = rest[:t], rest[t], rest[t + 1], rest[t + 2 :]
    low = pairs[Q_END + t - 1]
    high = pairs[Q_END + t]

    @pl.when(high > low)
    def _():
        fill(everything, pool, received)

        def sink(i, _, values):
            for k in range(6):
                rows[k, pl.ds(pl.multiple_of(8 * i, 8), 8), :] = values[k]

        all_pairs(everything, pairs, Q_A, low, high, 0, scratch, sink)


def into(totals, pairs):
    def sink(_, inside, values):
        for u in range(8):
            s = pairs[Q_SLOT + inside[u]]
            for k in range(6):
                totals[k, pl.ds(s, 1), :] = totals[k, pl.ds(s, 1), :] + values[k][u : u + 1]

    return sink


def middle_kernel(pairs, tab, pool, *rest):
    received = rest[:BITS]
    early = rest[BITS : BITS + len(CAPS)]
    state, totals, everything, *scratch = rest[BITS + len(CAPS) :]
    fill(everything, pool, received)

    def settle(i, _):
        for k in range(8):
            s = 8 * i + k
            at = tab[T_FINAL + s]
            for c in range(ROWS):
                state[c, pl.ds(s, 1), :] = everything[c, pl.ds(at, 1), :]
        return 0

    lax.fori_loop(0, S // 8, settle, 0)
    totals[...] = jnp.zeros((6, S, BLK), jnp.float32)
    for t, rows in zip(CAPS, early):
        low = pairs[Q_END + t - 1]
        high = pairs[Q_END + t]

        def add(e, _, low=low, rows=rows):
            s = pairs[Q_SLOT + e]
            for k in range(6):
                totals[k, pl.ds(s, 1), :] = totals[k, pl.ds(s, 1), :] + rows[k, pl.ds(e - low, 1), :]
            return 0

        lax.fori_loop(low, high, add, 0)
    low, high = pairs[Q_END + BITS - 1], pairs[Q_END + BITS]
    all_pairs(everything, pairs, Q_A, low, high, 0, scratch, into(totals, pairs))


def wide_kernel(pairs, state, wa, wb, totals_in, totals, everything, *scratch):
    totals[...] = totals_in[...]
    everything[:, 0:OWN, :] = state[...]
    everything[:, OWN : OWN + GHOST, :] = wa[:, 0:GHOST, :]
    everything[:, OWN + GHOST : OWN + 2 * GHOST, :] = wb[:, 0:GHOST, :]
    low, high = pairs[Q_END + 8], pairs[Q_END + 9]
    all_pairs(everything, pairs, Q_SLOT, low, high, GBASE - OWN, scratch, into(totals, pairs))


def last_kernel(pairs, state, la, lb, ca, cb, totals_in, pos, vel, spin, rad, totals, everything, *scratch):
    totals[...] = totals_in[...]
    everything[:, 0:OWN, :] = state[...]
    base = OWN - G_LA
    for at, part, n in ((G_LA, la, GHOST), (G_LB, lb, GHOST), (G_CA, ca, CORNERS), (G_CB, cb, CORNERS)):
        everything[:, base + at : base + at + n, :] = part[...]
    low, high = pairs[Q_END + 9], pairs[Q_END + 10]
    all_pairs(everything, pairs, Q_SLOT, low, high, GBASE - base, scratch, into(totals, pairs))
    a = state[9]
    mass = (DENSITY * (4.0 / 3.0) * math.pi) * a * a * a
    inertia = 0.4 * mass * a * a
    by_mass = TIME_STEP / mass
    by_inertia = TIME_STEP / inertia
    for c in range(3):
        v = state[3 + c] + totals[c] * by_mass
        vel[c] = v
        pos[c] = state[c] + TIME_STEP * v
        spin[c] = state[6 + c] + totals[3 + c] * by_inertia
    rad[...] = a


def neighbours(size, low):
    pairs = [(i, i + 1) for i in range(low, size - 1, 2)]
    return pairs + [(j, i) for i, j in pairs]


def kept(x):
    return pltpu.with_memory_space_constraint(x, pltpu.VMEM)


def stays(x):
    return pltpu.with_memory_space_constraint(x, pltpu.HBM)


def everything_of(rows):
    work = [pltpu.VMEM((ROWS, 8, BLK), jnp.float32)] * 2 + [pltpu.VMEM((64, BLK), jnp.int32)]
    return [pltpu.VMEM((ROWS, rows, BLK), jnp.float32)] + work


def body(
    positions,
    velocities,
    spins,
    sphere_radii,
    swap_counts,
    swap_slots,
    ghost_slots,
    corner_slots,
    pair_first,
    pair_second,
    pair_live,
):
    n_len = lax.axis_size("len")
    n_wid = lax.axis_size("wid")
    planes = [stays(x[0, 0].transpose(1, 0, 2)) for x in (positions, velocities, spins)]
    slots = swap_slots[0, 0]
    pool_t, send_t = vmem(ROWS, S, BLK), vmem(ROWS, MOVE, BLK)
    pool, send = call(
        pack_kernel,
        (pool_t, send_t),
        [HBM] * 5,
        (VMEM, VMEM),
        [pltpu.SMEM((BITS, MOVE), jnp.int32), pltpu.SemaphoreType.DMA((5,))],
        name="pack",
    )(stays(slots), *planes, stays(sphere_radii[0, 0]))
    pool = kept(pool)
    tab = call(
        table_kernel,
        jax.ShapeDtypeStruct((T_SIZE,), jnp.int32),
        [SMEM] * 4,
        SMEM,
        [pltpu.SMEM((S,), jnp.int32)],
        name="tables",
        flops=2000000,
    )(swap_counts[0, 0], slots, ghost_slots[0, 0], corner_slots[0, 0])
    pairs = call(
        order_kernel,
        jax.ShapeDtypeStruct((Q_SIZE,), jnp.int32),
        [SMEM] * 4,
        SMEM,
        [pltpu.SMEM((PAIRS,), jnp.int32), pltpu.SMEM((16,), jnp.int32)],
        name="order",
        flops=2000000,
    )(tab, pair_first[0, 0], pair_second[0, 0], pair_live)
    received, early = [], []
    behind = []
    for t in range(BITS):
        if t:
            send = call(
                functools.partial(step_kernel, t),
                send_t,
                [SMEM] + [VMEM] * (1 + t) + [ANY] * len(behind),
                VMEM,
                [pltpu.VMEM((ROWS, OWN + MOVE * t, BLK), jnp.float32)],
                name=f"step{t}",
            )(tab, pool, *received, *behind)
        axis, bit, size = ("len", t, n_len) if t < LBITS else ("wid", t - LBITS, n_wid)
        arrived = lax.ppermute(send, axis, [(i, i ^ (1 << bit)) for i in range(size)])
        behind = [pairs] if t == 1 else []
        if t in CAPS:
            rows = call(
                functools.partial(early_kernel, t),
                vmem(6, CAPS[t], BLK),
                [SMEM] + [VMEM] * (1 + t),
                VMEM,
                everything_of(OWN + MOVE * t),
                name=f"early{t}",
                flops=10000000,
            )(pairs, pool, *received)
            early.append(kept(rows))
            behind = early[-1:]
        received.append(kept(arrived))
    face_t, wide_t, corner_t = vmem(ROWS, GHOST, BLK), vmem(ROWS, WIDE, BLK), vmem(ROWS, CORNERS, BLK)
    la, lb, wa, wb = call(
        ghost_kernel,
        (face_t, face_t, wide_t, wide_t),
        [SMEM] + [VMEM] * (1 + BITS) + [ANY],
        (VMEM,) * 4,
        [pltpu.VMEM((ROWS, OWN + RECV, BLK), jnp.float32)],
        name="ghosts",
    )(tab, pool, *received, *behind)
    la = kept(lax.ppermute(la, "len", neighbours(n_len, 0)))
    lb = kept(lax.ppermute(lb, "len", neighbours(n_len, 1)))
    wa = kept(lax.ppermute(wa, "wid", neighbours(n_wid, 0)))
    wb = kept(lax.ppermute(wb, "wid", neighbours(n_wid, 1)))
    totals_t = vmem(6, S, BLK)
    state, totals = call(
        middle_kernel,
        (pool_t, totals_t),
        [SMEM] * 2 + [VMEM] * (1 + BITS + len(CAPS)),
        (VMEM, VMEM),
        everything_of(OWN + RECV),
        name="middle",
        flops=10000000,
    )(pairs, tab, pool, *received, *early)
    state, totals = kept(state), kept(totals)
    ca, cb = call(
        corner_kernel,
        (corner_t, corner_t),
        [VMEM] * 2 + [ANY],
        (VMEM, VMEM),
        name="corners",
    )(wa, wb, totals)
    ca = kept(lax.ppermute(ca, "len", neighbours(n_len, 0)))
    cb = kept(lax.ppermute(cb, "len", neighbours(n_len, 1)))
    totals = call(
        wide_kernel,
        totals_t,
        [SMEM] + [VMEM] * 4,
        VMEM,
        everything_of(OWN + 2 * GHOST),
        name="wide",
        flops=10000000,
    )(pairs, state, wa, wb, totals)
    out = call(
        last_kernel,
        (f32(3, S, BLK),) * 3 + (f32(S, BLK),),
        [SMEM] + [VMEM] * 6,
        (VMEM,) * 4,
        [pltpu.VMEM((6, S, BLK), jnp.float32)] + everything_of(OWN + 2 * GHOST + 2 * CORNERS),
        name="last",
    )(pairs, state, la, lb, ca, cb, kept(totals))
    outs = [x.transpose(1, 0, 2)[None, None] for x in out[:3]]
    return (*outs, out[3][None, None])


def solution(mesh):
    five = P("len", "wid", None, None, None)
    four = P("len", "wid", None, None)
    three = P("len", "wid", None)
    in_specs = (five, five, five, four, three, four, four, four, three, three, P("len", "wid"))
    out_specs = (five, five, five, four)
    return jax.shard_map(body, mesh=mesh, in_specs=in_specs, out_specs=out_specs, check_vma=False)
```

profile of v0, /device:TPU:193, one launch (start us, length us, event | category | flops | bytes accessed | tf_op | source)
XLA Modules:
  0.0 86.5 jit_solution(9018607756005715690)
XLA Ops:
  0.6 1.3 %pack.1 = (f32[10,192,128]{2,1,0:T(8,128)S(1)}, f32[10,24,128]{2,1,0:T(8,128)S(1)}) custom-call(s32[8,24]{1,0:T(8,128)} %bitcast.26, f32[3,192,128]{2,1,0:T(8,128)} %bitcast.33, f32[3,192,128]{2,1,0:T(8,128)} %bitcast.34, f32[3,192,128]{2,1,0:T(8,128)} %bitcast.35, f32[192,128]{1,0:T(8,128)} %bitcast.36), custom_call_target="tpu_custom_call" | custom-call | bytes 1000000 | tf_op jit(solution)/shard_map/pack/pallas_call | solution.py:484
  2.0 0.0 copy-start
  2.0 1.4 %collective-permute-start = (f32[10,24,128]{2,1,0:T(8,128)S(1)}, f32[10,24,128]{2,1,0:T(8,128)S(1)}, u32[]{:S(2)}, u32[]{:S(2)}) collective-permute-start(f32[10,24,128]{2,1,0:T(8,128)S(1)} %get-tuple-element.19), channel_id=1, source_target_pairs={{0,8},{8,0},{16,24},{24,16},{32,40},{40,32},{48,56},{56,48},{64,72... | collective-permute-start | bytes 368648 | tf_op jit(solution)/shard_map/ppermute | solution.py:524
  3.4 0.7 copy-done.1
  4.1 3.5 %tables.1.tab = s32[640]{0:T(1024)S(1)} custom-call(s32[8]{0:T(128)S(1)} %bitcast.30, s32[8,24]{1,0:T(8,128)S(1)} %bitcast.27, s32[4,48]{1,0:T(4,128)S(1)} %bitcast.28, s32[4,4]{1,0:T(4,128)S(1)} %bitcast.29), custom_call_target="tpu_custom_call" | custom-call | flops 2000000 | bytes 1000000 | tf_op jit(solution)/shard_map/tables/pallas_call | solution.py:493
  7.6 0.0 collective-permute-done.rest_0_
  7.6 0.7 step1.1
  8.3 2.7 %collective-permute-start.1 = (f32[10,24,128]{2,1,0:T(8,128)S(1)}, f32[10,24,128]{2,1,0:T(8,128)S(1)}, u32[]{:S(2)}, u32[]{:S(2)}) collective-permute-start(f32[10,24,128]{2,1,0:T(8,128)S(1)} %step1.1), channel_id=1, source_target_pairs={{0,16},{8,24},{16,0},{24,8},{32,48},{40,56},{48,32},{56,40},{64,80... | collective-permute-start | bytes 368648 | tf_op jit(solution)/shard_map/ppermute | solution.py:524
  11.7 0.0 copy-start.4
  11.7 0.0 copy-start.5
  11.7 0.6 copy-done.4
  12.3 0.0 copy-done.5
  12.3 5.3 %order.1.rest_2_.pairs = s32[512]{0:T(512)S(1)} custom-call(s32[640]{0:T(1024)S(1)} %tables.1.tab, s32[128]{0:T(128)S(1)} %bitcast.31, s32[128]{0:T(128)S(1)} %bitcast.32, s32[1,1]{1,0:T(1,128)S(6)} %copy.15.live_ref), custom_call_target="tpu_custom_call" | custom-call | flops 2000000 | bytes 1000000 | tf_op jit(solution)/shard_map/order/pallas_call | solution.py:502
  17.7 0.7 step2.1
  18.4 0.1 collective-permute-start.2
  18.5 2.3 %early2.1.rest_3_.rest_8_ = f32[6,16,128]{2,1,0:T(8,128)S(1)} custom-call(s32[512]{0:T(512)S(1)} %order.1.rest_2_.pairs, f32[10,192,128]{2,1,0:T(8,128)S(1)} %get-tuple-element.18.pool, f32[10,24,128]{2,1,0:T(8,128)S(1)} %collective-permute-done.rest_0_, f32[10,24,128]{2,1,0:T(8,128)S(1)} %collective-permute-done.1.rest_1_), custom_call_target="tpu_custom_call" | custom-call | flops 10000000 | bytes 1000000 | tf_op jit(solution)/shard_map/early2/pallas_call | solution.py:527
  20.9 1.4 %collective-permute-done.2.rest_2_ = f32[10,24,128]{2,1,0:T(8,128)S(1)} collective-permute-done((f32[10,24,128]{2,1,0:T(8,128)S(1)}, f32[10,24,128]{2,1,0:T(8,128)S(1)}, u32[]{:S(2)}, u32[]{:S(2)}) %collective-permute-start.2) | collective-permute-done | bytes 122912 | tf_op jit(solution)/shard_map/ppermute | solution.py:524
  22.2 0.7 step3.1
  23.0 1.6 %collective-permute-start.3 = (f32[10,24,128]{2,1,0:T(8,128)S(1)}, f32[10,24,128]{2,1,0:T(8,128)S(1)}, u32[]{:S(2)}, u32[]{:S(2)}) collective-permute-start(f32[10,24,128]{2,1,0:T(8,128)S(1)} %step3.1), channel_id=1, source_target_pairs={{0,64},{8,72},{16,80},{24,88},{32,96},{40,104},{48,112},{56,120},{... | collective-permute-start | bytes 368648 | tf_op jit(solution)/shard_map/ppermute | solution.py:524
  24.6 1.5 %early3.1.rest_4_.rest_9_ = f32[6,32,128]{2,1,0:T(8,128)S(1)} custom-call(s32[512]{0:T(512)S(1)} %order.1.rest_2_.pairs, f32[10,192,128]{2,1,0:T(8,128)S(1)} %get-tuple-element.18.pool, f32[10,24,128]{2,1,0:T(8,128)S(1)} %collective-permute-done.rest_0_, f32[10,24,128]{2,1,0:T(8,128)S(1)} %collective-permute-done.1.rest_1_, ...), custom_call_target="tpu_custom_call" | custom-call | flops 10000000 | bytes 1000000 | tf_op jit(solution)/shard_map/early3/pallas_call | solution.py:527
  26.1 4.1 %collective-permute-done.3.rest_3_ = f32[10,24,128]{2,1,0:T(8,128)S(1)} collective-permute-done((f32[10,24,128]{2,1,0:T(8,128)S(1)}, f32[10,24,128]{2,1,0:T(8,128)S(1)}, u32[]{:S(2)}, u32[]{:S(2)}) %collective-permute-start.3) | collective-permute-done | bytes 122912 | tf_op jit(solution)/shard_map/ppermute | solution.py:524
  30.2 0.8 step4.1
  31.0 0.1 collective-permute-start.4
  31.1 1.5 %early4.1.rest_5_.rest_10_ = f32[6,32,128]{2,1,0:T(8,128)S(1)} custom-call(s32[512]{0:T(512)S(1)} %order.1.rest_2_.pairs, f32[10,192,128]{2,1,0:T(8,128)S(1)} %get-tuple-element.18.pool, f32[10,24,128]{2,1,0:T(8,128)S(1)} %collective-permute-done.rest_0_, f32[10,24,128]{2,1,0:T(8,128)S(1)} %collective-permute-done.1.rest_1_, ...), custom_call_target="tpu_custom_call" | custom-call | flops 10000000 | bytes 1000000 | tf_op jit(solution)/shard_map/early4/pallas_call | solution.py:527
  32.7 6.2 %collective-permute-done.4.rest_4_ = f32[10,24,128]{2,1,0:T(8,128)S(1)} collective-permute-done((f32[10,24,128]{2,1,0:T(8,128)S(1)}, f32[10,24,128]{2,1,0:T(8,128)S(1)}, u32[]{:S(2)}, u32[]{:S(2)}) %collective-permute-start.4) | collective-permute-done | bytes 122912 | tf_op jit(solution)/shard_map/ppermute | solution.py:524
  38.9 0.8 step5.1
  39.6 2.1 %collective-permute-start.5 = (f32[10,24,128]{2,1,0:T(8,128)S(1)}, f32[10,24,128]{2,1,0:T(8,128)S(1)}, u32[]{:S(2)}, u32[]{:S(2)}) collective-permute-start(f32[10,24,128]{2,1,0:T(8,128)S(1)} %step5.1), channel_id=1, source_target_pairs={{0,1},{1,0},{2,3},{3,2},{4,5},{5,4},{6,7},{7,6},{8,9},{9,8},{10,11... | collective-permute-start | bytes 368648 | tf_op jit(solution)/shard_map/ppermute | solution.py:524
  41.7 1.0 %collective-permute-done.5.rest_5_ = f32[10,24,128]{2,1,0:T(8,128)S(1)} collective-permute-done((f32[10,24,128]{2,1,0:T(8,128)S(1)}, f32[10,24,128]{2,1,0:T(8,128)S(1)}, u32[]{:S(2)}, u32[]{:S(2)}) %collective-permute-start.5) | collective-permute-done | bytes 122912 | tf_op jit(solution)/shard_map/ppermute | solution.py:524
  42.7 0.8 step6.1
  43.5 0.3 collective-permute-start.6
  43.8 2.5 %early6.1.rest_7_.rest_11_ = f32[6,24,128]{2,1,0:T(8,128)S(1)} custom-call(s32[512]{0:T(512)S(1)} %order.1.rest_2_.pairs, f32[10,192,128]{2,1,0:T(8,128)S(1)} %get-tuple-element.18.pool, f32[10,24,128]{2,1,0:T(8,128)S(1)} %collective-permute-done.rest_0_, f32[10,24,128]{2,1,0:T(8,128)S(1)} %collective-permute-done.1.rest_1_, ...), custom_call_target="tpu_custom_call" | custom-call | flops 10000000 | bytes 1000000 | tf_op jit(solution)/shard_map/early6/pallas_call | solution.py:527
  46.3 1.8 %collective-permute-done.6.rest_6_ = f32[10,24,128]{2,1,0:T(8,128)S(1)} collective-permute-done((f32[10,24,128]{2,1,0:T(8,128)S(1)}, f32[10,24,128]{2,1,0:T(8,128)S(1)}, u32[]{:S(2)}, u32[]{:S(2)}) %collective-permute-start.6) | collective-permute-done | bytes 122912 | tf_op jit(solution)/shard_map/ppermute | solution.py:524
  48.1 0.8 step7.1
  48.9 3.8 %collective-permute-start.7 = (f32[10,24,128]{2,1,0:T(8,128)S(1)}, f32[10,24,128]{2,1,0:T(8,128)S(1)}, u32[]{:S(2)}, u32[]{:S(2)}) collective-permute-start(f32[10,24,128]{2,1,0:T(8,128)S(1)} %step7.1), channel_id=1, source_target_pairs={{0,4},{1,5},{2,6},{3,7},{4,0},{5,1},{6,2},{7,3},{8,12},{9,13},{10,... | collective-permute-start | bytes 368648 | tf_op jit(solution)/shard_map/ppermute | solution.py:524
  52.7 1.7 %early7.1.rest_12_.rest_8_ = f32[6,24,128]{2,1,0:T(8,128)S(1)} custom-call(s32[512]{0:T(512)S(1)} %order.1.rest_2_.pairs, f32[10,192,128]{2,1,0:T(8,128)S(1)} %get-tuple-element.18.pool, f32[10,24,128]{2,1,0:T(8,128)S(1)} %collective-permute-done.rest_0_, f32[10,24,128]{2,1,0:T(8,128)S(1)} %collective-permute-done.1.rest_1_, ...), custom_call_target="tpu_custom_call" | custom-call | flops 10000000 | bytes 1000000 | tf_op jit(solution)/shard_map/early7/pallas_call | solution.py:527
  54.4 0.6 collective-permute-done.7.rest_7_
  54.9 1.8 %ghosts.1 = (f32[10,48,128]{2,1,0:T(8,128)S(1)}, f32[10,48,128]{2,1,0:T(8,128)S(1)}, f32[10,56,128]{2,1,0:T(8,128)S(1)}, f32[10,56,128]{2,1,0:T(8,128)S(1)}) custom-call(s32[640]{0:T(1024)S(1)} %tables.1.tab, f32[10,192,128]{2,1,0:T(8,128)S(1)} %get-tuple-element.18.pool, f32[10,24,128]{2,1,0:T(8,128)S(1)} %collective-permute-done.rest_0_, ...), custom_call_target="tpu_custom_call" | custom-call | bytes 1000000 | tf_op jit(solution)/shard_map/ghosts/pallas_call | solution.py:540
  56.7 2.2 %collective-permute-start.10 = (f32[10,56,128]{2,1,0:T(8,128)S(1)}, f32[10,56,128]{2,1,0:T(8,128)S(1)}, u32[]{:S(2)}, u32[]{:S(2)}) collective-permute-start(f32[10,56,128]{2,1,0:T(8,128)S(1)} %get-tuple-element.23), channel_id=1, source_target_pairs={{0,1},{2,3},{4,5},{6,7},{1,0},{3,2},{5,4},{7,6},{8,9},{10,11},{12,... | collective-permute-start | bytes 860168 | tf_op jit(solution)/shard_map/ppermute | solution.py:550
  58.9 1.9 %collective-permute-start.11 = (f32[10,56,128]{2,1,0:T(8,128)S(1)}, f32[10,56,128]{2,1,0:T(8,128)S(1)}, u32[]{:S(2)}, u32[]{:S(2)}) collective-permute-start(f32[10,56,128]{2,1,0:T(8,128)S(1)} %get-tuple-element.24), channel_id=1, source_target_pairs={{1,2},{3,4},{5,6},{2,1},{4,3},{6,5},{9,10},{11,12},{13,14},{10,9},... | collective-permute-start | bytes 860168 | tf_op jit(solution)/shard_map/ppermute | solution.py:551
  60.8 2.2 %collective-permute-start.8 = (f32[10,48,128]{2,1,0:T(8,128)S(1)}, f32[10,48,128]{2,1,0:T(8,128)S(1)}, u32[]{:S(2)}, u32[]{:S(2)}) collective-permute-start(f32[10,48,128]{2,1,0:T(8,128)S(1)} %get-tuple-element.21), channel_id=1, source_target_pairs={{0,8},{16,24},{32,40},{48,56},{64,72},{80,88},{96,104},{112,120},{... | collective-permute-start | bytes 737288 | tf_op jit(solution)/shard_map/ppermute | solution.py:548
  63.0 1.9 %collective-permute-start.9 = (f32[10,48,128]{2,1,0:T(8,128)S(1)}, f32[10,48,128]{2,1,0:T(8,128)S(1)}, u32[]{:S(2)}, u32[]{:S(2)}) collective-permute-start(f32[10,48,128]{2,1,0:T(8,128)S(1)} %get-tuple-element.22), channel_id=1, source_target_pairs={{8,16},{24,32},{40,48},{56,64},{72,80},{88,96},{104,112},{120,128}... | collective-permute-start | bytes 737288 | tf_op jit(solution)/shard_map/ppermute | solution.py:549
  65.0 3.3 %middle.1 = (f32[10,192,128]{2,1,0:T(8,128)S(1)}, f32[6,192,128]{2,1,0:T(8,128)S(1)}) custom-call(s32[512]{0:T(512)S(1)} %order.1.rest_2_.pairs, s32[640]{0:T(1024)S(1)} %tables.1.tab, f32[10,192,128]{2,1,0:T(8,128)S(1)} %get-tuple-element.18.pool, f32[10,24,128]{2,1,0:T(8,128)S(1)} %collective-permute-done.rest_0_, ...), custom_call_target="tpu_custom_call" | custom-call | flops 10000000 | bytes 1000000 | tf_op jit(solution)/shard_map/middle/pallas_call | solution.py:553
  68.2 0.0 collective-permute-done.10.wa
  68.2 0.0 collective-permute-done.11.wb
  68.3 1.1 %collective-permute-start.12 = (f32[10,8,128]{2,1,0:T(8,128)S(1)}, f32[10,8,128]{2,1,0:T(8,128)S(1)}, u32[]{:S(2)}, u32[]{:S(2)}) collective-permute-start(f32[10,8,128]{2,1,0:T(8,128)S(1)} %get-tuple-element.26), channel_id=1, source_target_pairs={{0,8},{16,24},{32,40},{48,56},{64,72},{80,88},{96,104},{112,120},{... | collective-permute-start | bytes 122888 | tf_op jit(solution)/shard_map/ppermute | solution.py:570
  69.4 5.3 %collective-permute-start.13 = (f32[10,8,128]{2,1,0:T(8,128)S(1)}, f32[10,8,128]{2,1,0:T(8,128)S(1)}, u32[]{:S(2)}, u32[]{:S(2)}) collective-permute-start(f32[10,8,128]{2,1,0:T(8,128)S(1)} %get-tuple-element.27), channel_id=1, source_target_pairs={{8,16},{24,32},{40,48},{56,64},{72,80},{88,96},{104,112},{120,128}... | collective-permute-start | bytes 122888 | tf_op jit(solution)/shard_map/ppermute | solution.py:571
  74.7 4.3 %wide.1.totals_in = f32[6,192,128]{2,1,0:T(8,128)S(1)} custom-call(s32[512]{0:T(512)S(1)} %order.1.rest_2_.pairs, f32[10,192,128]{2,1,0:T(8,128)S(1)} %get-tuple-element.20.state, f32[10,56,128]{2,1,0:T(8,128)S(1)} %collective-permute-done.10.wa, f32[10,56,128]{2,1,0:T(8,128)S(1)} %collective-permute-done.11.wb, f32[6,192,128]{2,1,0:T(8,128)S(1)} %get-tuple-element.25._.totals_in), custom_call_target="tpu_custom_call" | custom-call | flops 10000000 | bytes 1000000 | tf_op jit(solution)/shard_map/wide/pallas_call | solution.py:572
  79.1 7.5 %last.1 = (f32[3,192,128]{2,1,0:T(8,128)}, f32[3,192,128]{2,1,0:T(8,128)}, f32[3,192,128]{2,1,0:T(8,128)}, f32[192,128]{1,0:T(8,128)}) custom-call(s32[512]{0:T(512)S(1)} %order.1.rest_2_.pairs, f32[10,192,128]{2,1,0:T(8,128)S(1)} %get-tuple-element.20.state, f32[10,48,128]{2,1,0:T(8,128)S(1)} %collective-permute-done.8.la, ...), custom_call_target="tpu_custom_call" | custom-call | bytes 1000000 | tf_op jit(solution)/shard_map/last/pallas_call | solution.py:581
  (12 shorter events, 0.1 us)
Async XLA Ops:
  0.6 2.8 %copy-start.2 = (s32[1,1,4,4]{3,2,1,0:T(4,128)S(1)}, s32[1,1,4,4]{3,2,1,0:T(4,128)}, u32[]{:S(2)}) copy-start(s32[1,1,4,4]{3,2,1,0:T(4,128)} %param.18) | copy-start | bytes 196
  2.0 1.4 %copy-start = (s32[1,1,8,24]{3,2,1,0:T(8,128)S(1)}, s32[1,1,8,24]{3,2,1,0:T(8,128)}, u32[]{:S(2)}) copy-start(s32[1,1,8,24]{3,2,1,0:T(8,128)} %param.16) | copy-start | bytes 2308
  2.0 5.6 %collective-permute-start = (f32[10,24,128]{2,1,0:T(8,128)S(1)}, f32[10,24,128]{2,1,0:T(8,128)S(1)}, u32[]{:S(2)}, u32[]{:S(2)}) collective-permute-start(f32[10,24,128]{2,1,0:T(8,128)S(1)} %get-tuple-element.19), channel_id=1, source_target_pairs={{0,8},{8,0},{16,24},{24,16},{32,40},{40,32},{48,56},{56,48},{64,72... | collective-permute-start | bytes 368648 | tf_op jit(solution)/shard_map/ppermute | solution.py:524
  3.4 0.7 copy-start.1
  3.4 0.7 copy-start.3
  8.3 9.4 %collective-permute-start.1 = (f32[10,24,128]{2,1,0:T(8,128)S(1)}, f32[10,24,128]{2,1,0:T(8,128)S(1)}, u32[]{:S(2)}, u32[]{:S(2)}) collective-permute-start(f32[10,24,128]{2,1,0:T(8,128)S(1)} %step1.1), channel_id=1, source_target_pairs={{0,16},{8,24},{16,0},{24,8},{32,48},{40,56},{48,32},{56,40},{64,80... | collective-permute-start | bytes 368648 | tf_op jit(solution)/shard_map/ppermute | solution.py:524
  11.7 0.7 copy-start.4
  11.7 0.7 copy-start.5
  18.4 3.8 %collective-permute-start.2 = (f32[10,24,128]{2,1,0:T(8,128)S(1)}, f32[10,24,128]{2,1,0:T(8,128)S(1)}, u32[]{:S(2)}, u32[]{:S(2)}) collective-permute-start(f32[10,24,128]{2,1,0:T(8,128)S(1)} %step2.1), channel_id=1, source_target_pairs={{0,32},{8,40},{16,48},{24,56},{32,0},{40,8},{48,16},{56,24},{64,96... | collective-permute-start | bytes 368648 | tf_op jit(solution)/shard_map/ppermute | solution.py:524
  23.0 7.2 %collective-permute-start.3 = (f32[10,24,128]{2,1,0:T(8,128)S(1)}, f32[10,24,128]{2,1,0:T(8,128)S(1)}, u32[]{:S(2)}, u32[]{:S(2)}) collective-permute-start(f32[10,24,128]{2,1,0:T(8,128)S(1)} %step3.1), channel_id=1, source_target_pairs={{0,64},{8,72},{16,80},{24,88},{32,96},{40,104},{48,112},{56,120},{... | collective-permute-start | bytes 368648 | tf_op jit(solution)/shard_map/ppermute | solution.py:524
  31.0 7.8 %collective-permute-start.4 = (f32[10,24,128]{2,1,0:T(8,128)S(1)}, f32[10,24,128]{2,1,0:T(8,128)S(1)}, u32[]{:S(2)}, u32[]{:S(2)}) collective-permute-start(f32[10,24,128]{2,1,0:T(8,128)S(1)} %step4.1), channel_id=1, source_target_pairs={{0,128},{8,136},{16,144},{24,152},{32,160},{40,168},{48,176},{56,1... | collective-permute-start | bytes 368648 | tf_op jit(solution)/shard_map/ppermute | solution.py:524
  39.6 3.1 %collective-permute-start.5 = (f32[10,24,128]{2,1,0:T(8,128)S(1)}, f32[10,24,128]{2,1,0:T(8,128)S(1)}, u32[]{:S(2)}, u32[]{:S(2)}) collective-permute-start(f32[10,24,128]{2,1,0:T(8,128)S(1)} %step5.1), channel_id=1, source_target_pairs={{0,1},{1,0},{2,3},{3,2},{4,5},{5,4},{6,7},{7,6},{8,9},{9,8},{10,11... | collective-permute-start | bytes 368648 | tf_op jit(solution)/shard_map/ppermute | solution.py:524
  43.5 4.6 %collective-permute-start.6 = (f32[10,24,128]{2,1,0:T(8,128)S(1)}, f32[10,24,128]{2,1,0:T(8,128)S(1)}, u32[]{:S(2)}, u32[]{:S(2)}) collective-permute-start(f32[10,24,128]{2,1,0:T(8,128)S(1)} %step6.1), channel_id=1, source_target_pairs={{0,2},{1,3},{2,0},{3,1},{4,6},{5,7},{6,4},{7,5},{8,10},{9,11},{10,... | collective-permute-start | bytes 368648 | tf_op jit(solution)/shard_map/ppermute | solution.py:524
  48.9 6.0 %collective-permute-start.7 = (f32[10,24,128]{2,1,0:T(8,128)S(1)}, f32[10,24,128]{2,1,0:T(8,128)S(1)}, u32[]{:S(2)}, u32[]{:S(2)}) collective-permute-start(f32[10,24,128]{2,1,0:T(8,128)S(1)} %step7.1), channel_id=1, source_target_pairs={{0,4},{1,5},{2,6},{3,7},{4,0},{5,1},{6,2},{7,3},{8,12},{9,13},{10,... | collective-permute-start | bytes 368648 | tf_op jit(solution)/shard_map/ppermute | solution.py:524
  56.7 11.5 %collective-permute-start.10 = (f32[10,56,128]{2,1,0:T(8,128)S(1)}, f32[10,56,128]{2,1,0:T(8,128)S(1)}, u32[]{:S(2)}, u32[]{:S(2)}) collective-permute-start(f32[10,56,128]{2,1,0:T(8,128)S(1)} %get-tuple-element.23), channel_id=1, source_target_pairs={{0,1},{2,3},{4,5},{6,7},{1,0},{3,2},{5,4},{7,6},{8,9},{10,11},{12,... | collective-permute-start | bytes 860168 | tf_op jit(solution)/shard_map/ppermute | solution.py:550
  58.9 9.3 %collective-permute-start.11 = (f32[10,56,128]{2,1,0:T(8,128)S(1)}, f32[10,56,128]{2,1,0:T(8,128)S(1)}, u32[]{:S(2)}, u32[]{:S(2)}) collective-permute-start(f32[10,56,128]{2,1,0:T(8,128)S(1)} %get-tuple-element.24), channel_id=1, source_target_pairs={{1,2},{3,4},{5,6},{2,1},{4,3},{6,5},{9,10},{11,12},{13,14},{10,9},... | collective-permute-start | bytes 860168 | tf_op jit(solution)/shard_map/ppermute | solution.py:551
  60.8 18.2 %collective-permute-start.8 = (f32[10,48,128]{2,1,0:T(8,128)S(1)}, f32[10,48,128]{2,1,0:T(8,128)S(1)}, u32[]{:S(2)}, u32[]{:S(2)}) collective-permute-start(f32[10,48,128]{2,1,0:T(8,128)S(1)} %get-tuple-element.21), channel_id=1, source_target_pairs={{0,8},{16,24},{32,40},{48,56},{64,72},{80,88},{96,104},{112,120},{... | collective-permute-start | bytes 737288 | tf_op jit(solution)/shard_map/ppermute | solution.py:548
  63.0 16.0 %collective-permute-start.9 = (f32[10,48,128]{2,1,0:T(8,128)S(1)}, f32[10,48,128]{2,1,0:T(8,128)S(1)}, u32[]{:S(2)}, u32[]{:S(2)}) collective-permute-start(f32[10,48,128]{2,1,0:T(8,128)S(1)} %get-tuple-element.22), channel_id=1, source_target_pairs={{8,16},{24,32},{40,48},{56,64},{72,80},{88,96},{104,112},{120,128}... | collective-permute-start | bytes 737288 | tf_op jit(solution)/shard_map/ppermute | solution.py:549
  68.3 10.8 %collective-permute-start.12 = (f32[10,8,128]{2,1,0:T(8,128)S(1)}, f32[10,8,128]{2,1,0:T(8,128)S(1)}, u32[]{:S(2)}, u32[]{:S(2)}) collective-permute-start(f32[10,8,128]{2,1,0:T(8,128)S(1)} %get-tuple-element.26), channel_id=1, source_target_pairs={{0,8},{16,24},{32,40},{48,56},{64,72},{80,88},{96,104},{112,120},{... | collective-permute-start | bytes 122888 | tf_op jit(solution)/shard_map/ppermute | solution.py:570
  69.4 9.7 %collective-permute-start.13 = (f32[10,8,128]{2,1,0:T(8,128)S(1)}, f32[10,8,128]{2,1,0:T(8,128)S(1)}, u32[]{:S(2)}, u32[]{:S(2)}) collective-permute-start(f32[10,8,128]{2,1,0:T(8,128)S(1)} %get-tuple-element.27), channel_id=1, source_target_pairs={{8,16},{24,32},{40,48},{56,64},{72,80},{88,96},{104,112},{120,128}... | collective-permute-start | bytes 122888 | tf_op jit(solution)/shard_map/ppermute | solution.py:571
where the time goes:
time: 87.6 us; the launch traced here: 86.5 us
  Pallas kernels  41.9 us (48%)
  starting transfers between devices  26.7 us (30%)
  waiting for transfers between devices  15 us (17%)
  between operations  1.58 us (2%)
  local copies, waits for them, and re-layouts  1.34 us (2%)
    ppermute x8, waiting for transfers between devices, body(): arrived = lax.ppermute(send, axis, [(i, i ^ 1 << bit) for i in range(size)])  15 us
    ppermute x8, starting transfers between devices, body(): arrived = lax.ppermute(send, axis, [(i, i ^ 1 << bit) for i in range(size)])  12.1 us
    pallas_call x5, Pallas kernels, body(): call(functools.partial(early_kernel, t), vmem(6, CAPS[t], BLK), [SMEM] +...  9.52 us
    pallas_call x1, Pallas kernels, body(): call(last_kernel, (f32(3, S, BLK),) * 3 + (f32(S, BLK),), [SMEM] + [VMEM]...  7.45 us
    pallas_call x7, Pallas kernels, body(): call(functools.partial(step_kernel, t), send_t, [SMEM] + [VMEM] * (1 + t)...  5.34 us
    pallas_call x1, Pallas kernels, body(): call(order_kernel, jax.ShapeDtypeStruct((Q_SIZE,), jnp.int32), [SMEM] * 4...  5.31 us
    ppermute x1, starting transfers between devices, body(): cb = kept(lax.ppermute(cb, 'len', neighbours(n_len, 1)))  5.29 us
    pallas_call x1, Pallas kernels, body(): call(wide_kernel, totals_t, [SMEM] + [VMEM] * 4, VMEM, everything_of(OWN...  4.35 us
  transfers between devices with their start and end apart: 14, of which 6 were waited for; matrix products, arithmetic and copies ran while one was open for 0% of the time, Pallas kernels for 30%

commit v1 on v0

--- a/solution.py
+++ b/solution.py
@@ -23,13 +23,14 @@
 RECV = MOVE * BITS
 WIDE = GHOST + 2 * CORNER
 CORNERS = 2 * CORNER
-G_WA, G_WB, G_LA, G_LB, G_CA, G_CB = 0, GHOST, 2 * GHOST, 3 * GHOST, 4 * GHOST, 4 * GHOST + CORNERS
+G_WA, G_WB, G_LA, G_LB = 0, GHOST, 2 * GHOST, 2 * GHOST + WIDE
 GBASE = OWN + RECV
-T_SEND, T_FINAL, T_GHOST, T_CORNER = 0, 192, 384, 576
-T_SIZE = 640
+T_SEND, T_FINAL, T_SIZE = 0, 192, 512
+G_FACE, G_CORNER, G_SIZE = 0, 192, 256
+C_CAT, C_START, C_END, C_SIZE = 0, 128, 144, 256
 Q_A, Q_B, Q_SLOT, Q_END = 0, 136, 272, 408
 Q_SIZE = 512
-CAPS = {2: 16, 3: 32, 4: 32, 6: 24, 7: 24}
+CAPS = {3: 32, 4: 40, 6: 24, 7: 24}
 CATS = 12
 SPARE = 11
 MARGIN = 0.02
@@ -45,11 +46,15 @@
     return jax.ShapeDtypeStruct(shape, jnp.float32)
 
 
+def ints(size):
+    return jax.ShapeDtypeStruct((size,), jnp.int32)
+
+
 def vmem(*shape):
     return pltpu.VMEM(shape, jnp.float32)
 
 
-def call(body, out_shape, in_specs, out_specs, scratch=(), name=None, flops=0):
+def call(body, out_shape, in_specs, out_specs, scratch=(), name=None, flops=0, aliases=None):
     return pl.pallas_call(
         body,
         out_shape=out_shape,
@@ -57,6 +62,7 @@
         out_specs=out_specs,
         scratch_shapes=list(scratch),
         name=name,
+        input_output_aliases=aliases or {},
         compiler_params=pltpu.CompilerParams(vmem_limit_bytes=24 * 1024 * 1024),
         cost_estimate=pl.CostEstimate(flops=flops, transcendentals=0, bytes_accessed=1000000),
     )
@@ -80,10 +86,10 @@
             send[c, j : j + 1, :] = pool[c, pl.ds(s, 1), :]
 
 
-def table_kernel(counts, slots, ghosts, corners, tab, code):
+def table_kernel(counts, slots, tab):
     def init(i, _):
         for k in range(16):
-            code[16 * i + k] = 16 * i + k
+            tab[T_FINAL + 16 * i + k] = 16 * i + k
         return 0
 
     lax.fori_loop(0, S // 16, init, 0)
@@ -94,12 +100,12 @@
         def one(i, _):
             first = 8 * i
             places = [slots[t, first + k] for k in range(8)]
-            olds = [code[s] for s in places]
+            olds = [tab[T_FINAL + s] for s in places]
             for k in range(8):
                 tab[T_SEND + MOVE * t + first + k] = olds[k]
             for k in range(8):
                 j = first + k
-                code[places[k]] = jnp.where(j < live, S + MOVE * t + j, olds[k])
+                tab[T_FINAL + places[k]] = jnp.where(j < live, S + MOVE * t + j, olds[k])
             return 0
 
         lax.fori_loop(0, MOVE // 8, one, 0)
@@ -107,33 +113,25 @@
 
     lax.fori_loop(0, BITS, move, 0)
 
-    def final(i, _):
-        values = [code[8 * i + k] for k in range(8)]
-        for k in range(8):
-            tab[T_FINAL + 8 * i + k] = values[k]
-        return 0
-
-    lax.fori_loop(0, S // 8, final, 0)
+
+def ghost_table_kernel(tab, ghosts, corners, out):
     for k in range(4):
 
         def face(i, _, k=k):
-            values = [code[ghosts[k, 8 * i + g]] for g in range(8)]
+            values = [tab[T_FINAL + ghosts[k, 8 * i + g]] for g in range(8)]
             for g in range(8):
-                tab[T_GHOST + GHOST * k + 8 * i + g] = values[g]
+                out[G_FACE + GHOST * k + 8 * i + g] = values[g]
             return 0
 
         lax.fori_loop(0, GHOST // 8, face, 0)
         for g in range(CORNER):
-            tab[T_CORNER + CORNER * k + g] = code[corners[k, g]]
-
-
-def order_kernel(tab, first, second, live_ref, out, cat, start):
+            out[G_CORNER + CORNER * k + g] = tab[T_FINAL + corners[k, g]]
+
+
+def count_kernel(tab, first, second, live_ref, out, start):
     live = live_ref[0, 0]
-    even_w = odd("wid") == 0
-    even_l = odd("len") == 0
     for k in range(CATS):
         start[k] = 0
-    groups = (live + 3) // 4
 
     def sort_in(i, _):
         cats = []
@@ -147,23 +145,31 @@
             where = jnp.where(b < S, ready, jnp.where(wide, 9, 10))
             cats.append(jnp.where(e < live, where, SPARE))
         for k in range(4):
-            cat[4 * i + k] = cats[k]
+            out[C_CAT + 4 * i + k] = cats[k]
         for k in range(4):
             start[cats[k]] = start[cats[k]] + 1
         return 0
 
-    lax.fori_loop(0, groups, sort_in, 0)
+    lax.fori_loop(0, (live + 3) // 4, sort_in, 0)
     total = jnp.int32(0)
     done = jnp.int32(0)
     for k in range(CATS):
-        n = start[k]
-        start[k] = total
-        total = total + n
+        out[C_START + k] = total
+        total = total + start[k]
         if k < BITS:
             done = jnp.minimum(total, done + CAPS.get(k, 0))
-            out[Q_END + k] = done
+            out[C_END + k] = done
         else:
-            out[Q_END + k] = total
+            out[C_END + k] = total
+
+
+def place_kernel(tab, cats, first, second, live_ref, out, start):
+    live = live_ref[0, 0]
+    even_w = odd("wid") == 0
+    even_l = late() == 0
+    for k in range(CATS):
+        start[k] = cats[C_START + k]
+        out[Q_END + k] = cats[C_END + k]
 
     def place(i, _):
         spots = []
@@ -178,11 +184,12 @@
             low = jnp.where(diagonal, h < 2 * CORNER, face < 2)
             wide = (face == 1) | (face == 2)
             ahead = jnp.where(wide & (h < 0), low == even_w, low == even_l)
-            start_at = jnp.where(wide, G_WA, G_LA) + jnp.where(ahead, 0, GHOST) + g - face * GHOST
-            corner_at = G_CA + jnp.where(ahead, 0, CORNERS) + h - jnp.where(low, 0, CORNERS)
-            ghost = jnp.where(diagonal, corner_at, start_at) + GBASE
+            wide_at = jnp.where(ahead, G_WA, G_WB) + g - face * GHOST
+            inside = jnp.where(diagonal, GHOST + h - jnp.where(low, 0, CORNERS), g - face * GHOST)
+            long_at = jnp.where(ahead, G_LA, G_LB) + inside
+            ghost = jnp.where(wide & (h < 0), wide_at, long_at) + GBASE
             own = tab[T_FINAL + jnp.minimum(b, S - 1)]
-            spots.append((cat[e], a, tab[T_FINAL + a], jnp.where(b < S, own, ghost)))
+            spots.append((cats[C_CAT + e], a, tab[T_FINAL + a], jnp.where(b < S, own, ghost)))
         for where, a, near, far in spots:
             at = start[where]
             start[where] = at + 1
@@ -191,7 +198,7 @@
             out[Q_B + at] = far
         return 0
 
-    lax.fori_loop(0, groups, place, 0)
+    lax.fori_loop(0, (live + 3) // 4, place, 0)
 
 
 def gather_rows(everything, tab, base, count, out, at):
@@ -217,30 +224,38 @@
     return lax.rem(lax.axis_index(axis), 2)
 
 
-def ghost_kernel(tab, pool, *rest):
-    received = rest[:BITS]
-    la, lb, wa, wb, everything = rest[-5:]
-    fill(everything, pool, received)
+def late():
+    return lax.rem(lax.axis_index("len") + lax.axis_index("wid"), 2)
+
+
+def wide_faces_kernel(tab, pool, *rest):
+    wa, wb, everything = rest[-3:]
+    fill(everything, pool, rest[:BITS])
     up = 1 - odd("wid")
     for out, k in ((wa, up), (wb, 1 - up)):
-        gather_rows(everything, tab, T_GHOST + GHOST * (1 + k), GHOST, out, 0)
-        gather_rows(everything, tab, T_CORNER + CORNER * k, CORNER, out, GHOST)
-        gather_rows(everything, tab, T_CORNER + CORNER * (2 + k), CORNER, out, GHOST + CORNER)
-    up = 1 - odd("len")
+        gather_rows(everything, tab, G_FACE + GHOST * (1 + k), GHOST, out, 0)
+        gather_rows(everything, tab, G_CORNER + CORNER * k, CORNER, out, GHOST)
+        gather_rows(everything, tab, G_CORNER + CORNER * (2 + k), CORNER, out, GHOST + CORNER)
+
+
+def long_faces_kernel(tab, pool, *rest):
+    la, lb, everything = rest[-3:]
+    fill(everything, pool, rest[:BITS])
+    up = 1 - late()
     for out, k in ((la, up), (lb, 1 - up)):
-        gather_rows(everything, tab, T_GHOST + 3 * GHOST * k, GHOST, out, 0)
-
-
-def corner_kernel(wa, wb, _, ca, cb):
-    up = 1 - odd("len")
+        gather_rows(everything, tab, G_FACE + 3 * GHOST * k, GHOST, out, 0)
+
+
+def forward_kernel(wa, wb, _, la_in, lb_in, la, lb):
+    up = 1 - late()
     flip = odd("wid")
     swap = jnp.full((CORNER, BLK), flip) == 1
-    for out, k in ((ca, up), (cb, 1 - up)):
+    for out, k in ((la, up), (lb, 1 - up)):
         for c in range(ROWS):
             at = pl.ds(GHOST + CORNER * k, CORNER)
             a, b = wa[c, at, :], wb[c, at, :]
-            out[c, 0:CORNER, :] = jnp.where(swap, b, a)
-            out[c, CORNER:CORNERS, :] = jnp.where(swap, a, b)
+            out[c, GHOST : GHOST + CORNER, :] = jnp.where(swap, b, a)
+            out[c, GHOST + CORNER : WIDE, :] = jnp.where(swap, a, b)
 
 
 def rounded(x):
@@ -424,14 +439,14 @@
     all_pairs(everything, pairs, Q_SLOT, low, high, GBASE - OWN, scratch, into(totals, pairs))
 
 
-def last_kernel(pairs, state, la, lb, ca, cb, totals_in, pos, vel, spin, rad, totals, everything, *scratch):
+def last_kernel(pairs, state, la, lb, totals_in, pos, vel, spin, rad, totals, everything, *scratch):
     totals[...] = totals_in[...]
     everything[:, 0:OWN, :] = state[...]
-    base = OWN - G_LA
-    for at, part, n in ((G_LA, la, GHOST), (G_LB, lb, GHOST), (G_CA, ca, CORNERS), (G_CB, cb, CORNERS)):
-        everything[:, base + at : base + at + n, :] = part[...]
+    everything[:, OWN : OWN + WIDE, :] = la[...]
+    everything[:, OWN + WIDE : OWN + 2 * WIDE, :] = lb[...]
     low, high = pairs[Q_END + 9], pairs[Q_END + 10]
-    all_pairs(everything, pairs, Q_SLOT, low, high, GBASE - base, scratch, into(totals, pairs))
+    shift = GBASE + G_LA - OWN
+    all_pairs(everything, pairs, Q_SLOT, low, high, shift, scratch, into(totals, pairs))
     a = state[9]
     mass = (DENSITY * (4.0 / 3.0) * math.pi) * a * a * a
     inertia = 0.4 * mass * a * a
@@ -448,6 +463,16 @@
 def neighbours(size, low):
     pairs = [(i, i + 1) for i in range(low, size - 1, 2)]
     return pairs + [(j, i) for i, j in pairs]
+
+
+def long_neighbours(n_len, n_wid, second):
+    route = []
+    for i in range(n_len):
+        for w in range(n_wid):
+            j = i + 1 if (i + w + second) % 2 == 0 else i - 1
+            if 0 <= j < n_len:
+                route.append((i * n_wid + w, j * n_wid + w))
+    return route
 
 
 def kept(x):
@@ -490,24 +515,19 @@
         name="pack",
     )(stays(slots), *planes, stays(sphere_radii[0, 0]))
     pool = kept(pool)
-    tab = call(
-        table_kernel,
-        jax.ShapeDtypeStruct((T_SIZE,), jnp.int32),
-        [SMEM] * 4,
-        SMEM,
-        [pltpu.SMEM((S,), jnp.int32)],
-        name="tables",
-        flops=2000000,
-    )(swap_counts[0, 0], slots, ghost_slots[0, 0], corner_slots[0, 0])
-    pairs = call(
-        order_kernel,
-        jax.ShapeDtypeStruct((Q_SIZE,), jnp.int32),
-        [SMEM] * 4,
-        SMEM,
-        [pltpu.SMEM((PAIRS,), jnp.int32), pltpu.SMEM((16,), jnp.int32)],
-        name="order",
-        flops=2000000,
-    )(tab, pair_first[0, 0], pair_second[0, 0], pair_live)
+    lists = (pair_first[0, 0], pair_second[0, 0], pair_live)
+    counter = [pltpu.SMEM((16,), jnp.int32)]
+    tab = call(table_kernel, ints(T_SIZE), [SMEM] * 2, SMEM, name="tables", flops=2000000)(
+        swap_counts[0, 0], slots
+    )
+    cats = call(count_kernel, ints(C_SIZE), [SMEM] * 4, SMEM, counter, "count", 2000000)(tab, *lists)
+    pairs = call(place_kernel, ints(Q_SIZE), [SMEM] * 5, SMEM, counter, "place", 2000000)(
+        tab, cats, *lists
+    )
+    gtab = call(ghost_table_kernel, ints(G_SIZE), [SMEM] * 3, SMEM, name="ghost_table", flops=1000000)(
+        tab, ghost_slots[0, 0], corner_slots[0, 0]
+    )
+    windows = {1: [cats], 2: [pairs], 4: [gtab]}
     received, early = [], []
     behind = []
     for t in range(BITS):
@@ -522,7 +542,7 @@
             )(tab, pool, *received, *behind)
         axis, bit, size = ("len", t, n_len) if t < LBITS else ("wid", t - LBITS, n_wid)
         arrived = lax.ppermute(send, axis, [(i, i ^ (1 << bit)) for i in range(size)])
-        behind = [pairs] if t == 1 else []
+        behind = list(windows.get(t, []))
         if t in CAPS:
             rows = call(
                 functools.partial(early_kernel, t),
@@ -534,21 +554,30 @@
                 flops=10000000,
             )(pairs, pool, *received)
             early.append(kept(rows))
-            behind = early[-1:]
+            behind.append(early[-1])
         received.append(kept(arrived))
-    face_t, wide_t, corner_t = vmem(ROWS, GHOST, BLK), vmem(ROWS, WIDE, BLK), vmem(ROWS, CORNERS, BLK)
-    la, lb, wa, wb = call(
-        ghost_kernel,
-        (face_t, face_t, wide_t, wide_t),
-        [SMEM] + [VMEM] * (1 + BITS) + [ANY],
-        (VMEM,) * 4,
-        [pltpu.VMEM((ROWS, OWN + RECV, BLK), jnp.float32)],
-        name="ghosts",
-    )(tab, pool, *received, *behind)
-    la = kept(lax.ppermute(la, "len", neighbours(n_len, 0)))
-    lb = kept(lax.ppermute(lb, "len", neighbours(n_len, 1)))
+    wide_t = vmem(ROWS, WIDE, BLK)
+    faces = [pltpu.VMEM((ROWS, OWN + RECV, BLK), jnp.float32)]
+    wa, wb = call(
+        wide_faces_kernel,
+        (wide_t, wide_t),
+        [SMEM] + [VMEM] * (1 + BITS) + [ANY] * len(behind),
+        (VMEM, VMEM),
+        faces,
+        name="wide_faces",
+    )(gtab, pool, *received, *behind)
+    sent = kept(wa)
     wa = kept(lax.ppermute(wa, "wid", neighbours(n_wid, 0)))
     wb = kept(lax.ppermute(wb, "wid", neighbours(n_wid, 1)))
+    la, lb = call(
+        long_faces_kernel,
+        (wide_t, wide_t),
+        [SMEM] + [VMEM] * (1 + BITS) + [ANY],
+        (VMEM, VMEM),
+        faces,
+        name="long_faces",
+        flops=1000000,
+    )(gtab, pool, *received, sent)
     totals_t = vmem(6, S, BLK)
     state, totals = call(
         middle_kernel,
@@ -560,15 +589,16 @@
         flops=10000000,
     )(pairs, tab, pool, *received, *early)
     state, totals = kept(state), kept(totals)
-    ca, cb = call(
-        corner_kernel,
-        (corner_t, corner_t),
-        [VMEM] * 2 + [ANY],
+    la, lb = call(
+        forward_kernel,
+        (wide_t, wide_t),
+        [VMEM] * 2 + [ANY] + [VMEM] * 2,
         (VMEM, VMEM),
-        name="corners",
-    )(wa, wb, totals)
-    ca = kept(lax.ppermute(ca, "len", neighbours(n_len, 0)))
-    cb = kept(lax.ppermute(cb, "len", neighbours(n_len, 1)))
+        name="forward",
+        aliases={3: 0, 4: 1},
+    )(wa, wb, totals, kept(la), kept(lb))
+    la = kept(lax.ppermute(la, ("len", "wid"), long_neighbours(n_len, n_wid, 0)))
+    lb = kept(lax.ppermute(lb, ("len", "wid"), long_neighbours(n_len, n_wid, 1)))
     totals = call(
         wide_kernel,
         totals_t,
@@ -581,11 +611,11 @@
     out = call(
         last_kernel,
         (f32(3, S, BLK),) * 3 + (f32(S, BLK),),
-        [SMEM] + [VMEM] * 6,
+        [SMEM] + [VMEM] * 4,
         (VMEM,) * 4,
-        [pltpu.VMEM((6, S, BLK), jnp.float32)] + everything_of(OWN + 2 * GHOST + 2 * CORNERS),
+        [pltpu.VMEM((6, S, BLK), jnp.float32)] + everything_of(OWN + 2 * WIDE),
         name="last",
-    )(pairs, state, la, lb, ca, cb, kept(totals))
+    )(pairs, state, la, lb, kept(totals))
     outs = [x.transpose(1, 0, 2)[None, None] for x in out[:3]]
     return (*outs, out[3][None, None])
 

time: 87.6 us -> 83.9 us (0.958)
  the two profiles are of different devices: /device:TPU:193 before, /device:TPU:228 now
where the time goes in v1:
time: 83.9 us; the launch traced here: 82.8 us
  Pallas kernels  36.6 us (44%)
  waiting for transfers between devices  24.6 us (29%)
  starting transfers between devices  19.4 us (23%)
  between operations  1.56 us (2%)
    ppermute x8, waiting for transfers between devices, body(): arrived = lax.ppermute(send, axis, [(i, i ^ 1 << bit) for i in range(size)])  16.9 us
    ppermute x8, starting transfers between devices, body(): arrived = lax.ppermute(send, axis, [(i, i ^ 1 << bit) for i in range(size)])  11.3 us
    pallas_call x4, Pallas kernels, body(): call(functools.partial(early_kernel, t), vmem(6, CAPS[t], BLK), [SMEM] +...  7.74 us
    ppermute x1, waiting for transfers between devices, body(): lax.ppermute(lb, ('len', 'wid'), long_neighbours(n_len, n_wid, 1))  6.04 us
    pallas_call x7, Pallas kernels, body(): call(functools.partial(step_kernel, t), send_t, [SMEM] + [VMEM] * (1 + t)...  5.28 us
    pallas_call x1, Pallas kernels, body(): call(last_kernel, (f32(3, S, BLK),) * 3 + (f32(S, BLK),), [SMEM] + [VMEM]...  4.64 us
    ppermute x1, starting transfers between devices, body(): lax.ppermute(la, ('len', 'wid'), long_neighbours(n_len, n_wid, 0))  3.93 us
    pallas_call x1, Pallas kernels, body(): call(middle_kernel, (pool_t, totals_t), [SMEM] * 2 + [VMEM] * (1 + BITS +...  3.15 us
  transfers between devices with their start and end apart: 12, of which 9 were waited for; matrix products, arithmetic and copies ran while one was open for 0% of the time, Pallas kernels for 29%

profile of v1, /device:TPU:228, one launch (start us, length us, event | category | flops | bytes accessed | tf_op | source)
XLA Modules:
  0.0 82.8 jit_solution(9158053217313025609)
XLA Ops:
  0.6 1.3 %pack.1 = (f32[10,192,128]{2,1,0:T(8,128)S(1)}, f32[10,24,128]{2,1,0:T(8,128)S(1)}) custom-call(s32[8,24]{1,0:T(8,128)} %bitcast.26, f32[3,192,128]{2,1,0:T(8,128)} %bitcast.35, f32[3,192,128]{2,1,0:T(8,128)} %bitcast.36, f32[3,192,128]{2,1,0:T(8,128)} %bitcast.37, f32[192,128]{1,0:T(8,128)} %bitcast.38), custom_call_target="tpu_custom_call" | custom-call | bytes 1000000 | tf_op jit(solution)/shard_map/pack/pallas_call | solution.py:509
  2.0 0.0 copy-start.3
  2.0 1.7 %collective-permute-start = (f32[10,24,128]{2,1,0:T(8,128)S(1)}, f32[10,24,128]{2,1,0:T(8,128)S(1)}, u32[]{:S(2)}, u32[]{:S(2)}) collective-permute-start(f32[10,24,128]{2,1,0:T(8,128)S(1)} %get-tuple-element.19), channel_id=1, source_target_pairs={{0,8},{8,0},{16,24},{24,16},{32,40},{40,32},{48,56},{56,48},{64,72... | collective-permute-start | bytes 368648 | tf_op jit(solution)/shard_map/ppermute | solution.py:544
  3.7 2.6 %tables.1.tab = s32[512]{0:T(512)S(1)} custom-call(s32[8]{0:T(128)S(1)} %bitcast.30, s32[8,24]{1,0:T(8,128)S(1)} %bitcast.27), custom_call_target="tpu_custom_call" | custom-call | flops 2000000 | bytes 1000000 | tf_op jit(solution)/shard_map/tables/pallas_call | solution.py:520
  6.3 0.9 %collective-permute-done.rest_0_ = f32[10,24,128]{2,1,0:T(8,128)S(1)} collective-permute-done((f32[10,24,128]{2,1,0:T(8,128)S(1)}, f32[10,24,128]{2,1,0:T(8,128)S(1)}, u32[]{:S(2)}, u32[]{:S(2)}) %collective-permute-start) | collective-permute-done | bytes 122912 | tf_op jit(solution)/shard_map/ppermute | solution.py:544
  7.1 0.7 step1.1
  7.9 3.3 %collective-permute-start.1 = (f32[10,24,128]{2,1,0:T(8,128)S(1)}, f32[10,24,128]{2,1,0:T(8,128)S(1)}, u32[]{:S(2)}, u32[]{:S(2)}) collective-permute-start(f32[10,24,128]{2,1,0:T(8,128)S(1)} %step1.1), channel_id=1, source_target_pairs={{0,16},{8,24},{16,0},{24,8},{32,48},{40,56},{48,32},{56,40},{64,80... | collective-permute-start | bytes 368648 | tf_op jit(solution)/shard_map/ppermute | solution.py:544
  11.8 0.0 copy-start.4
  11.8 0.0 copy-start.5
  11.8 0.6 copy-done.4
  12.5 0.0 copy-done.5
  12.5 2.0 %count.1.cats.rest_2_ = s32[256]{0:T(256)S(1)} custom-call(s32[512]{0:T(512)S(1)} %tables.1.tab, s32[128]{0:T(128)S(1)} %bitcast.31, s32[128]{0:T(128)S(1)} %bitcast.33, s32[1,1]{1,0:T(1,128)S(6)} %copy.19.live_ref), custom_call_target="tpu_custom_call" | custom-call | flops 2000000 | bytes 1000000 | tf_op jit(solution)/shard_map/count/pallas_call | solution.py:523
  14.5 0.7 step2.1
  15.2 1.0 %collective-permute-start.2 = (f32[10,24,128]{2,1,0:T(8,128)S(1)}, f32[10,24,128]{2,1,0:T(8,128)S(1)}, u32[]{:S(2)}, u32[]{:S(2)}) collective-permute-start(f32[10,24,128]{2,1,0:T(8,128)S(1)} %step2.1), channel_id=1, source_target_pairs={{0,32},{8,40},{16,48},{24,56},{32,0},{40,8},{48,16},{56,24},{64,96... | collective-permute-start | bytes 368648 | tf_op jit(solution)/shard_map/ppermute | solution.py:544
  16.2 3.1 %place.1.rest_3_.pairs = s32[512]{0:T(512)S(1)} custom-call(s32[512]{0:T(512)S(1)} %tables.1.tab, s32[256]{0:T(256)S(1)} %count.1.cats.rest_2_, s32[128]{0:T(128)S(1)} %bitcast.32, s32[128]{0:T(128)S(1)} %bitcast.34, s32[1,1]{1,0:T(1,128)S(6)} %copy.19.live_ref), custom_call_target="tpu_custom_call" | custom-call | flops 2000000 | bytes 1000000 | tf_op jit(solution)/shard_map/place/pallas_call | solution.py:524
  19.2 0.9 %collective-permute-done.2.rest_2_ = f32[10,24,128]{2,1,0:T(8,128)S(1)} collective-permute-done((f32[10,24,128]{2,1,0:T(8,128)S(1)}, f32[10,24,128]{2,1,0:T(8,128)S(1)}, u32[]{:S(2)}, u32[]{:S(2)}) %collective-permute-start.2) | collective-permute-done | bytes 122912 | tf_op jit(solution)/shard_map/ppermute | solution.py:544
  20.2 0.7 step3.1
  20.9 1.4 %collective-permute-start.3 = (f32[10,24,128]{2,1,0:T(8,128)S(1)}, f32[10,24,128]{2,1,0:T(8,128)S(1)}, u32[]{:S(2)}, u32[]{:S(2)}) collective-permute-start(f32[10,24,128]{2,1,0:T(8,128)S(1)} %step3.1), channel_id=1, source_target_pairs={{0,64},{8,72},{16,80},{24,88},{32,96},{40,104},{48,112},{56,120},{... | collective-permute-start | bytes 368648 | tf_op jit(solution)/shard_map/ppermute | solution.py:544
  22.3 2.3 %early3.1.rest_4_.rest_8_ = f32[6,32,128]{2,1,0:T(8,128)S(1)} custom-call(s32[512]{0:T(512)S(1)} %place.1.rest_3_.pairs, f32[10,192,128]{2,1,0:T(8,128)S(1)} %get-tuple-element.18.pool, f32[10,24,128]{2,1,0:T(8,128)S(1)} %collective-permute-done.rest_0_, f32[10,24,128]{2,1,0:T(8,128)S(1)} %collective-permute-done.1.rest_1_, ...), custom_call_target="tpu_custom_call" | custom-call | flops 10000000 | bytes 1000000 | tf_op jit(solution)/shard_map/early3/pallas_call | solution.py:547
  24.7 3.5 %collective-permute-done.3.rest_3_ = f32[10,24,128]{2,1,0:T(8,128)S(1)} collective-permute-done((f32[10,24,128]{2,1,0:T(8,128)S(1)}, f32[10,24,128]{2,1,0:T(8,128)S(1)}, u32[]{:S(2)}, u32[]{:S(2)}) %collective-permute-start.3) | collective-permute-done | bytes 122912 | tf_op jit(solution)/shard_map/ppermute | solution.py:544
  28.2 0.8 step4.1
  29.0 1.3 %collective-permute-start.4 = (f32[10,24,128]{2,1,0:T(8,128)S(1)}, f32[10,24,128]{2,1,0:T(8,128)S(1)}, u32[]{:S(2)}, u32[]{:S(2)}) collective-permute-start(f32[10,24,128]{2,1,0:T(8,128)S(1)} %step4.1), channel_id=1, source_target_pairs={{0,128},{8,136},{16,144},{24,152},{32,160},{40,168},{48,176},{56,1... | collective-permute-start | bytes 368648 | tf_op jit(solution)/shard_map/ppermute | solution.py:544
  30.3 1.9 %ghost_table.1.rest_5_.tab = s32[256]{0:T(256)S(1)} custom-call(s32[512]{0:T(512)S(1)} %tables.1.tab, s32[4,48]{1,0:T(4,128)S(1)} %bitcast.28, s32[4,4]{1,0:T(4,128)S(1)} %bitcast.29), custom_call_target="tpu_custom_call" | custom-call | flops 1000000 | bytes 1000000 | tf_op jit(solution)/shard_map/ghost_table/pallas_call | solution.py:527
  32.2 1.5 %early4.1.rest_6_.rest_9_ = f32[6,40,128]{2,1,0:T(8,128)S(1)} custom-call(s32[512]{0:T(512)S(1)} %place.1.rest_3_.pairs, f32[10,192,128]{2,1,0:T(8,128)S(1)} %get-tuple-element.18.pool, f32[10,24,128]{2,1,0:T(8,128)S(1)} %collective-permute-done.rest_0_, f32[10,24,128]{2,1,0:T(8,128)S(1)} %collective-permute-done.1.rest_1_, ...), custom_call_target="tpu_custom_call" | custom-call | flops 10000000 | bytes 1000000 | tf_op jit(solution)/shard_map/early4/pallas_call | solution.py:547
  33.7 4.1 %collective-permute-done.4.rest_4_ = f32[10,24,128]{2,1,0:T(8,128)S(1)} collective-permute-done((f32[10,24,128]{2,1,0:T(8,128)S(1)}, f32[10,24,128]{2,1,0:T(8,128)S(1)}, u32[]{:S(2)}, u32[]{:S(2)}) %collective-permute-start.4) | collective-permute-done | bytes 122912 | tf_op jit(solution)/shard_map/ppermute | solution.py:544
  37.9 0.8 step5.1
  38.7 0.1 collective-permute-start.5
  38.8 1.3 %collective-permute-done.5.rest_5_ = f32[10,24,128]{2,1,0:T(8,128)S(1)} collective-permute-done((f32[10,24,128]{2,1,0:T(8,128)S(1)}, f32[10,24,128]{2,1,0:T(8,128)S(1)}, u32[]{:S(2)}, u32[]{:S(2)}) %collective-permute-start.5) | collective-permute-done | bytes 122912 | tf_op jit(solution)/shard_map/ppermute | solution.py:544
  40.1 0.8 step6.1
  40.9 2.5 %collective-permute-start.6 = (f32[10,24,128]{2,1,0:T(8,128)S(1)}, f32[10,24,128]{2,1,0:T(8,128)S(1)}, u32[]{:S(2)}, u32[]{:S(2)}) collective-permute-start(f32[10,24,128]{2,1,0:T(8,128)S(1)} %step6.1), channel_id=1, source_target_pairs={{0,2},{1,3},{2,0},{3,1},{4,6},{5,7},{6,4},{7,5},{8,10},{9,11},{10,... | collective-permute-start | bytes 368648 | tf_op jit(solution)/shard_map/ppermute | solution.py:544
  43.3 1.5 %early6.1.rest_7_.rest_10_ = f32[6,24,128]{2,1,0:T(8,128)S(1)} custom-call(s32[512]{0:T(512)S(1)} %place.1.rest_3_.pairs, f32[10,192,128]{2,1,0:T(8,128)S(1)} %get-tuple-element.18.pool, f32[10,24,128]{2,1,0:T(8,128)S(1)} %collective-permute-done.rest_0_, f32[10,24,128]{2,1,0:T(8,128)S(1)} %collective-permute-done.1.rest_1_, ...), custom_call_target="tpu_custom_call" | custom-call | flops 10000000 | bytes 1000000 | tf_op jit(solution)/shard_map/early6/pallas_call | solution.py:547
  44.8 2.1 %collective-permute-done.6.rest_6_ = f32[10,24,128]{2,1,0:T(8,128)S(1)} collective-permute-done((f32[10,24,128]{2,1,0:T(8,128)S(1)}, f32[10,24,128]{2,1,0:T(8,128)S(1)}, u32[]{:S(2)}, u32[]{:S(2)}) %collective-permute-start.6) | collective-permute-done | bytes 122912 | tf_op jit(solution)/shard_map/ppermute | solution.py:544
  47.0 0.8 step7.1
  47.7 0.1 collective-permute-start.7
  47.8 2.4 %early7.1.rest_11_.rest_8_ = f32[6,24,128]{2,1,0:T(8,128)S(1)} custom-call(s32[512]{0:T(512)S(1)} %place.1.rest_3_.pairs, f32[10,192,128]{2,1,0:T(8,128)S(1)} %get-tuple-element.18.pool, f32[10,24,128]{2,1,0:T(8,128)S(1)} %collective-permute-done.rest_0_, f32[10,24,128]{2,1,0:T(8,128)S(1)} %collective-permute-done.1.rest_1_, ...), custom_call_target="tpu_custom_call" | custom-call | flops 10000000 | bytes 1000000 | tf_op jit(solution)/shard_map/early7/pallas_call | solution.py:547
  50.2 4.0 %collective-permute-done.7.rest_7_ = f32[10,24,128]{2,1,0:T(8,128)S(1)} collective-permute-done((f32[10,24,128]{2,1,0:T(8,128)S(1)}, f32[10,24,128]{2,1,0:T(8,128)S(1)}, u32[]{:S(2)}, u32[]{:S(2)}) %collective-permute-start.7) | collective-permute-done | bytes 122912 | tf_op jit(solution)/shard_map/ppermute | solution.py:544
  54.2 1.3 %wide_faces.1 = (f32[10,56,128]{2,1,0:T(8,128)S(1)}, f32[10,56,128]{2,1,0:T(8,128)S(1)}) custom-call(s32[256]{0:T(256)S(1)} %ghost_table.1.rest_5_.tab, f32[10,192,128]{2,1,0:T(8,128)S(1)} %get-tuple-element.18.pool, f32[10,24,128]{2,1,0:T(8,128)S(1)} %collective-permute-done.rest_0_, f32[10,24,128]{2,1,0:T(8,128)S(1)} %collective-permute-done.1.rest_1_, ...), custom_call_target="tpu_custom_call" | custom-call | bytes 1000000 | tf_op jit(solution)/shard_map/wide_faces/pallas_call | solution.py:561
  55.5 0.1 collective-permute-start.8
  55.6 2.0 %collective-permute-start.9 = (f32[10,56,128]{2,1,0:T(8,128)S(1)}, f32[10,56,128]{2,1,0:T(8,128)S(1)}, u32[]{:S(2)}, u32[]{:S(2)}) collective-permute-start(f32[10,56,128]{2,1,0:T(8,128)S(1)} %get-tuple-element.22), channel_id=1, source_target_pairs={{1,2},{3,4},{5,6},{2,1},{4,3},{6,5},{9,10},{11,12},{13,14},{10,9},... | collective-permute-start | bytes 860168 | tf_op jit(solution)/shard_map/ppermute | solution.py:571
  57.6 1.2 %long_faces.1 = (f32[10,56,128]{2,1,0:T(8,128)S(1)}, f32[10,56,128]{2,1,0:T(8,128)S(1)}) custom-call(s32[256]{0:T(256)S(1)} %ghost_table.1.rest_5_.tab, f32[10,192,128]{2,1,0:T(8,128)S(1)} %get-tuple-element.18.pool, f32[10,24,128]{2,1,0:T(8,128)S(1)} %collective-permute-done.rest_0_, f32[10,24,128]{2,1,0:T(8,128)S(1)} %collective-permute-done.1.rest_1_, ...), custom_call_target="tpu_custom_call" | custom-call | flops 1000000 | bytes 1000000 | tf_op jit(solution)/shard_map/long_faces/pallas_call | solution.py:572
  58.8 3.2 %middle.1 = (f32[10,192,128]{2,1,0:T(8,128)S(1)}, f32[6,192,128]{2,1,0:T(8,128)S(1)}) custom-call(s32[512]{0:T(512)S(1)} %place.1.rest_3_.pairs, s32[512]{0:T(512)S(1)} %tables.1.tab, f32[10,192,128]{2,1,0:T(8,128)S(1)} %get-tuple-element.18.pool, f32[10,24,128]{2,1,0:T(8,128)S(1)} %collective-permute-done.rest_0_, ...), custom_call_target="tpu_custom_call" | custom-call | flops 10000000 | bytes 1000000 | tf_op jit(solution)/shard_map/middle/pallas_call | solution.py:582
  62.0 1.5 %collective-permute-done.9.wb = f32[10,56,128]{2,1,0:T(8,128)S(1)} collective-permute-done((f32[10,56,128]{2,1,0:T(8,128)S(1)}, f32[10,56,128]{2,1,0:T(8,128)S(1)}, u32[]{:S(2)}, u32[]{:S(2)}) %collective-permute-start.9) | collective-permute-done | bytes 286752 | tf_op jit(solution)/shard_map/ppermute | solution.py:571
  63.6 3.9 %collective-permute-start.10 = (f32[10,56,128]{2,1,0:T(8,128)S(1)}, f32[10,56,128]{2,1,0:T(8,128)S(1)}, u32[]{:S(2)}, u32[]{:S(2)}) collective-permute-start(f32[10,56,128]{2,1,0:T(8,128)S(1)} %get-tuple-element.26), channel_id=1, source_target_pairs={{0,8},{2,10},{4,12},{6,14},{8,0},{9,17},{10,2},{11,19},{12,4},{13,... | collective-permute-start | bytes 860168 | tf_op jit(solution)/shard_map/ppermute | solution.py:600
  67.5 2.0 %collective-permute-start.11 = (f32[10,56,128]{2,1,0:T(8,128)S(1)}, f32[10,56,128]{2,1,0:T(8,128)S(1)}, u32[]{:S(2)}, u32[]{:S(2)}) collective-permute-start(f32[10,56,128]{2,1,0:T(8,128)S(1)} %get-tuple-element.27), channel_id=1, source_target_pairs={{1,9},{3,11},{5,13},{7,15},{8,16},{9,1},{10,18},{11,3},{12,20},{13... | collective-permute-start | bytes 860168 | tf_op jit(solution)/shard_map/ppermute | solution.py:601
  69.5 2.5 %wide.1.totals_in = f32[6,192,128]{2,1,0:T(8,128)S(1)} custom-call(s32[512]{0:T(512)S(1)} %place.1.rest_3_.pairs, f32[10,192,128]{2,1,0:T(8,128)S(1)} %get-tuple-element.20.state, f32[10,56,128]{2,1,0:T(8,128)S(1)} %collective-permute-done.8.wa, f32[10,56,128]{2,1,0:T(8,128)S(1)} %collective-permute-done.9.wb, f32[6,192,128]{2,1,0:T(8,128)S(1)} %get-tuple-element.23._.totals_in), custom_call_target="tpu_custom_call" | custom-call | flops 10000000 | bytes 1000000 | tf_op jit(solution)/shard_map/wide/pallas_call | solution.py:602
  72.1 0.0 collective-permute-done.10.la
  72.1 6.0 %collective-permute-done.11.lb = f32[10,56,128]{2,1,0:T(8,128)S(1)} collective-permute-done((f32[10,56,128]{2,1,0:T(8,128)S(1)}, f32[10,56,128]{2,1,0:T(8,128)S(1)}, u32[]{:S(2)}, u32[]{:S(2)}) %collective-permute-start.11) | collective-permute-done | bytes 286752 | tf_op jit(solution)/shard_map/ppermute | solution.py:601
  78.1 4.6 %last.1 = (f32[3,192,128]{2,1,0:T(8,128)}, f32[3,192,128]{2,1,0:T(8,128)}, f32[3,192,128]{2,1,0:T(8,128)}, f32[192,128]{1,0:T(8,128)}) custom-call(s32[512]{0:T(512)S(1)} %place.1.rest_3_.pairs, f32[10,192,128]{2,1,0:T(8,128)S(1)} %get-tuple-element.20.state, f32[10,56,128]{2,1,0:T(8,128)S(1)} %collective-permute-done.10.la, ...), custom_call_target="tpu_custom_call" | custom-call | bytes 1000000 | tf_op jit(solution)/shard_map/last/pallas_call | solution.py:611
  (10 shorter events, 0.0 us)
Async XLA Ops:
  0.6 3.0 %copy-start = (s32[1,1,8,24]{3,2,1,0:T(8,128)S(1)}, s32[1,1,8,24]{3,2,1,0:T(8,128)}, u32[]{:S(2)}) copy-start(s32[1,1,8,24]{3,2,1,0:T(8,128)} %param.16) | copy-start | bytes 2308
  2.0 1.7 %copy-start.3 = (s32[1,1,8]{2,1,0:T(1,128)S(1)}, s32[1,1,8]{2,1,0:T(1,128)}, u32[]{:S(2)}) copy-start(s32[1,1,8]{2,1,0:T(1,128)} %param.15) | copy-start | bytes 100
  2.0 5.1 %collective-permute-start = (f32[10,24,128]{2,1,0:T(8,128)S(1)}, f32[10,24,128]{2,1,0:T(8,128)S(1)}, u32[]{:S(2)}, u32[]{:S(2)}) collective-permute-start(f32[10,24,128]{2,1,0:T(8,128)S(1)} %get-tuple-element.19), channel_id=1, source_target_pairs={{0,8},{8,0},{16,24},{24,16},{32,40},{40,32},{48,56},{56,48},{64,72... | collective-permute-start | bytes 368648 | tf_op jit(solution)/shard_map/ppermute | solution.py:544
  7.9 6.6 %collective-permute-start.1 = (f32[10,24,128]{2,1,0:T(8,128)S(1)}, f32[10,24,128]{2,1,0:T(8,128)S(1)}, u32[]{:S(2)}, u32[]{:S(2)}) collective-permute-start(f32[10,24,128]{2,1,0:T(8,128)S(1)} %step1.1), channel_id=1, source_target_pairs={{0,16},{8,24},{16,0},{24,8},{32,48},{40,56},{48,32},{56,40},{64,80... | collective-permute-start | bytes 368648 | tf_op jit(solution)/shard_map/ppermute | solution.py:544
  11.8 0.7 copy-start.4
  11.8 0.7 copy-start.5
  15.2 5.0 %collective-permute-start.2 = (f32[10,24,128]{2,1,0:T(8,128)S(1)}, f32[10,24,128]{2,1,0:T(8,128)S(1)}, u32[]{:S(2)}, u32[]{:S(2)}) collective-permute-start(f32[10,24,128]{2,1,0:T(8,128)S(1)} %step2.1), channel_id=1, source_target_pairs={{0,32},{8,40},{16,48},{24,56},{32,0},{40,8},{48,16},{56,24},{64,96... | collective-permute-start | bytes 368648 | tf_op jit(solution)/shard_map/ppermute | solution.py:544
  20.9 7.3 %collective-permute-start.3 = (f32[10,24,128]{2,1,0:T(8,128)S(1)}, f32[10,24,128]{2,1,0:T(8,128)S(1)}, u32[]{:S(2)}, u32[]{:S(2)}) collective-permute-start(f32[10,24,128]{2,1,0:T(8,128)S(1)} %step3.1), channel_id=1, source_target_pairs={{0,64},{8,72},{16,80},{24,88},{32,96},{40,104},{48,112},{56,120},{... | collective-permute-start | bytes 368648 | tf_op jit(solution)/shard_map/ppermute | solution.py:544
  28.2 2.1 %copy-start.2 = (s32[1,1,4,4]{3,2,1,0:T(4,128)S(1)}, s32[1,1,4,4]{3,2,1,0:T(4,128)}, u32[]{:S(2)}) copy-start(s32[1,1,4,4]{3,2,1,0:T(4,128)} %param.18) | copy-start | bytes 196
  29.0 1.3 %copy-start.1 = (s32[1,1,4,48]{3,2,1,0:T(4,128)S(1)}, s32[1,1,4,48]{3,2,1,0:T(4,128)}, u32[]{:S(2)}) copy-start(s32[1,1,4,48]{3,2,1,0:T(4,128)} %param.17) | copy-start | bytes 2308
  29.0 8.9 %collective-permute-start.4 = (f32[10,24,128]{2,1,0:T(8,128)S(1)}, f32[10,24,128]{2,1,0:T(8,128)S(1)}, u32[]{:S(2)}, u32[]{:S(2)}) collective-permute-start(f32[10,24,128]{2,1,0:T(8,128)S(1)} %step4.1), channel_id=1, source_target_pairs={{0,128},{8,136},{16,144},{24,152},{32,160},{40,168},{48,176},{56,1... | collective-permute-start | bytes 368648 | tf_op jit(solution)/shard_map/ppermute | solution.py:544
  38.7 1.4 %collective-permute-start.5 = (f32[10,24,128]{2,1,0:T(8,128)S(1)}, f32[10,24,128]{2,1,0:T(8,128)S(1)}, u32[]{:S(2)}, u32[]{:S(2)}) collective-permute-start(f32[10,24,128]{2,1,0:T(8,128)S(1)} %step5.1), channel_id=1, source_target_pairs={{0,1},{1,0},{2,3},{3,2},{4,5},{5,4},{6,7},{7,6},{8,9},{9,8},{10,11... | collective-permute-start | bytes 368648 | tf_op jit(solution)/shard_map/ppermute | solution.py:544
  40.9 6.1 %collective-permute-start.6 = (f32[10,24,128]{2,1,0:T(8,128)S(1)}, f32[10,24,128]{2,1,0:T(8,128)S(1)}, u32[]{:S(2)}, u32[]{:S(2)}) collective-permute-start(f32[10,24,128]{2,1,0:T(8,128)S(1)} %step6.1), channel_id=1, source_target_pairs={{0,2},{1,3},{2,0},{3,1},{4,6},{5,7},{6,4},{7,5},{8,10},{9,11},{10,... | collective-permute-start | bytes 368648 | tf_op jit(solution)/shard_map/ppermute | solution.py:544
  47.7 6.5 %collective-permute-start.7 = (f32[10,24,128]{2,1,0:T(8,128)S(1)}, f32[10,24,128]{2,1,0:T(8,128)S(1)}, u32[]{:S(2)}, u32[]{:S(2)}) collective-permute-start(f32[10,24,128]{2,1,0:T(8,128)S(1)} %step7.1), channel_id=1, source_target_pairs={{0,4},{1,5},{2,6},{3,7},{4,0},{5,1},{6,2},{7,3},{8,12},{9,13},{10,... | collective-permute-start | bytes 368648 | tf_op jit(solution)/shard_map/ppermute | solution.py:544
  55.5 6.5 %collective-permute-start.8 = (f32[10,56,128]{2,1,0:T(8,128)S(1)}, f32[10,56,128]{2,1,0:T(8,128)S(1)}, u32[]{:S(2)}, u32[]{:S(2)}) collective-permute-start(f32[10,56,128]{2,1,0:T(8,128)S(1)} %get-tuple-element.21.rest_8_), channel_id=1, source_target_pairs={{0,1},{2,3},{4,5},{6,7},{1,0},{3,2},{5,4},{7,6},{8,9},{10,11},{12,... | collective-permute-start | bytes 860168 | tf_op jit(solution)/shard_map/ppermute | solution.py:570
  55.6 8.0 %collective-permute-start.9 = (f32[10,56,128]{2,1,0:T(8,128)S(1)}, f32[10,56,128]{2,1,0:T(8,128)S(1)}, u32[]{:S(2)}, u32[]{:S(2)}) collective-permute-start(f32[10,56,128]{2,1,0:T(8,128)S(1)} %get-tuple-element.22), channel_id=1, source_target_pairs={{1,2},{3,4},{5,6},{2,1},{4,3},{6,5},{9,10},{11,12},{13,14},{10,9},... | collective-permute-start | bytes 860168 | tf_op jit(solution)/shard_map/ppermute | solution.py:571
  63.6 8.5 %collective-permute-start.10 = (f32[10,56,128]{2,1,0:T(8,128)S(1)}, f32[10,56,128]{2,1,0:T(8,128)S(1)}, u32[]{:S(2)}, u32[]{:S(2)}) collective-permute-start(f32[10,56,128]{2,1,0:T(8,128)S(1)} %get-tuple-element.26), channel_id=1, source_target_pairs={{0,8},{2,10},{4,12},{6,14},{8,0},{9,17},{10,2},{11,19},{12,4},{13,... | collective-permute-start | bytes 860168 | tf_op jit(solution)/shard_map/ppermute | solution.py:600
  67.5 10.6 %collective-permute-start.11 = (f32[10,56,128]{2,1,0:T(8,128)S(1)}, f32[10,56,128]{2,1,0:T(8,128)S(1)}, u32[]{:S(2)}, u32[]{:S(2)}) collective-permute-start(f32[10,56,128]{2,1,0:T(8,128)S(1)} %get-tuple-element.27), channel_id=1, source_target_pairs={{1,9},{3,11},{5,13},{7,15},{8,16},{9,1},{10,18},{11,3},{12,20},{13... | collective-permute-start | bytes 860168 | tf_op jit(solution)/shard_map/ppermute | solution.py:601
